TPU v7x, 32 devices: a whole 2x2x4 slice. The times are simulated.
32 devices in a mesh: groups: 1, wide: 32 (over z, y, x, core).
Axes of the slice: x: 2, y: 2, z: 4, core: 2. Of those that a mesh axis runs over, the one named last changes fastest.
Arguments:
- queries: bfloat16 [256, 1152], P('groups'), may hold values from -4 to 4
- patch_keys: bfloat16 [4096, 1152], P(('groups', 'wide')), may hold values from -173 to 173
- patch_values: bfloat16 [4096, 2560], P(('groups', 'wide')), may hold values from -6 to 6
- norm_gain: float32 [2560], replicated, may hold values from 0.1 to 1.9
- route_experts: int32 [512, 6], P(('groups', 'wide')), may hold values from 0 to 15, all different within a row; in each aligned block of 16 rows (0 to 15, 16 to 31, ...) at most 16 rows name the same one
- route_weights: int32 [512, 6], P(('groups', 'wide')), may hold values from 1 to 16
- w_gate: bfloat16 [16384, 2560], P('wide'), may hold values from -0.125 to 0.125
- w_up: bfloat16 [16384, 2560], P('wide'), may hold values from -0.125 to 0.125
- w_down: bfloat16 [16384, 2560], P('wide'), may hold values from -0.1875 to 0.1875
Outputs:
- mixed_rows: bfloat16 [512, 2560], P(('groups', 'wide'))
Inputs may be any that keep to these rules, and one draw needn't show every extreme that they name: `route_experts`: each row names 6 different experts. In each aligned block of 16 rows (the rows of one device) no expert is named by more than 16 rows, a bound that some block reaches.
All inputs are finite; a program needn't handle non-finite values.
Results may differ from a plain program's by a relative error of at most 0.02.
Values may be sent and summed in bfloat16 or wider, within the bound.
No kernel may reach another device: no remote copies, remote signals or barrier semaphores. Data moves between devices by JAX's collectives and lax.ppermute only.
A program may use at most 128 MiB of HBM per device.

v0:
```python
import jax
import jax.numpy as jnp
from jax import lax
from jax.sharding import PartitionSpec as P

HEADS = 16


def partner(value, axis, stride):
    mask = 2**stride
    pairs = [(source, source ^ mask) for source in range(lax.axis_size(axis))]
    return lax.ppermute(value, axis, pairs)


def merge_partials(first_part, second_part, head_count):
    sum_first, peak_first, total_first = first_part
    sum_second, peak_second, total_second = second_part
    row_peak = jnp.maximum(peak_first, peak_second)
    factor_first = jnp.exp(peak_first - row_peak)
    factor_second = jnp.exp(peak_second - row_peak)
    row_total = total_first * factor_first + total_second * factor_second
    row_count = sum_first.shape[0]
    summed = sum_first.reshape(row_count, head_count, -1) * factor_first[:, :, None]
    summed = summed + sum_second.reshape(row_count, head_count, -1) * factor_second[:, :, None]
    return (summed.reshape(row_count, -1), row_peak, row_total)


def on_device(
    queries, patch_keys, patch_values, norm_gain, route_experts, route_weights, w_gate, w_up, w_down
):
    row_count = route_experts.shape[0]
    top_k = route_experts.shape[1]
    model_width = patch_values.shape[1]
    vision_width = patch_keys.shape[1]
    head_count = HEADS
    key_size = vision_width // head_count
    value_size = model_width // head_count
    group_size = queries.shape[0] // row_count
    levels = group_size.bit_length() - 1
    devices = lax.axis_size("wide")
    device_index = lax.axis_index("wide")
    score_scale = key_size ** (-0.5)
    scores = (
        jnp.einsum(
            "qhc,phc->qhp",
            queries.reshape(-1, head_count, key_size),
            patch_keys.reshape(-1, head_count, key_size),
            preferred_element_type=jnp.float32,
        )
        * score_scale
    )
    row_peak = jnp.max(scores, axis=2)
    raised = jnp.exp(scores - row_peak[:, :, None])
    row_total = jnp.sum(raised, axis=2)
    summed = jnp.einsum(
        "qhp,phc->qhc",
        raised.astype(jnp.bfloat16),
        patch_values.reshape(-1, head_count, value_size),
        preferred_element_type=jnp.float32,
    ).reshape(-1, model_width)
    for bit_number in reversed(range(levels)):
        half_rows = summed.shape[0] // 2
        upper_half = device_index // (1 << bit_number) % 2 == 1
        kept_part = (
            jnp.where(upper_half, summed[half_rows:], summed[:half_rows]),
            jnp.where(upper_half, row_peak[half_rows:], row_peak[:half_rows]),
            jnp.where(upper_half, row_total[half_rows:], row_total[:half_rows]),
        )
        sent_sum = jnp.where(upper_half, summed[:half_rows], summed[half_rows:])
        sent_peak = jnp.where(upper_half, row_peak[:half_rows], row_peak[half_rows:])
        sent_total = jnp.where(upper_half, row_total[:half_rows], row_total[half_rows:])
        partner_part = partner((sent_sum, sent_peak, sent_total), "wide", bit_number)
        summed, row_peak, row_total = merge_partials(kept_part, partner_part, head_count)
    attended = summed.reshape(row_count, head_count, value_size) / row_total[:, :, None]
    projected = attended.reshape(row_count, model_width).astype(jnp.bfloat16)
    residual = projected.astype(jnp.float32)
    normed = (
        residual
        * lax.rsqrt(jnp.mean(residual * residual, axis=1, keepdims=True) + 1e-06)
        * norm_gain
    ).astype(jnp.bfloat16)
    experts = devices // 2
    capacity = 32 * row_count // devices
    flat_routes = route_experts.reshape(-1)
    onehot = (flat_routes[:, None] == jnp.arange(experts, dtype=jnp.int32)[None, :]).astype(
        jnp.int32
    )
    earlier = jnp.cumsum(onehot, axis=0) - onehot
    slot_index = jnp.sum(earlier * onehot, axis=1)
    position = flat_routes * capacity + slot_index
    placing = jnp.any(
        position.reshape(row_count, top_k)[:, :, None]
        == jnp.arange(experts * capacity, dtype=jnp.int32)[None, None, :],
        axis=1,
    )
    buffer = lax.dot_general(
        placing.astype(jnp.bfloat16),
        normed,
        (((0,), (0,)), ((), ())),
        preferred_element_type=jnp.float32,
    ).astype(jnp.bfloat16)
    sent_rows = jnp.broadcast_to(
        buffer.reshape(experts, 1, capacity, model_width), (experts, 2, capacity, model_width)
    ).reshape(devices, capacity, model_width)
    received = lax.all_to_all(sent_rows, "wide", split_axis=0, concat_axis=0, tiled=True)
    sources, item_count, row_width = received.shape
    flat_rows = received.reshape(sources * item_count, row_width)
    gate_part = lax.dot_general(
        w_gate, flat_rows, (((1,), (1,)), ((), ())), preferred_element_type=jnp.float32
    )
    up_part = lax.dot_general(
        w_up, flat_rows, (((1,), (1,)), ((), ())), preferred_element_type=jnp.float32
    )
    hidden = (jax.nn.silu(gate_part) * up_part).astype(jnp.bfloat16)
    partial_value = lax.dot_general(
        hidden, w_down, (((0,), (0,)), ((), ())), preferred_element_type=jnp.float32
    )
    partial_value = partial_value.reshape(sources, item_count, row_width)
    returned = lax.all_to_all(
        partial_value.astype(jnp.bfloat16), "wide", split_axis=0, concat_axis=0, tiled=True
    ).astype(partial_value.dtype)
    outputs = (
        jnp.sum(returned.reshape(experts, 2, -1, model_width), axis=1)
        .astype(jnp.bfloat16)
        .reshape(-1, model_width)
    )
    picked = (
        jnp.take(outputs, position, axis=0)
        .reshape(row_count, top_k, model_width)
        .astype(jnp.float32)
    )
    scores_int = route_weights.astype(jnp.float32)
    gate_share = scores_int / jnp.sum(scores_int, axis=1, keepdims=True)
    mixed_rows = residual + jnp.sum(picked * gate_share[:, :, None], axis=1)
    return mixed_rows.astype(jnp.bfloat16)


def solution(mesh):
    return jax.shard_map(
        on_device,
        mesh=mesh,
        in_specs=(
            P("groups", None),
            P(("groups", "wide"), None),
            P(("groups", "wide"), None),
            P(),
            P(("groups", "wide"), None),
            P(("groups", "wide"), None),
            P("wide", None),
            P("wide", None),
            P("wide", None),
        ),
        out_specs=P(("groups", "wide"), None),
        check_vma=False,
    )
```

profile of v0, /device:TPU:0, one launch (start us, length us, event | category | flops | bytes accessed | tf_op | source)
XLA Modules:
  0.0 246.2 jit_solution(1788478821131541885)
XLA Ops:
  4.9 3.1 %collective-permute-start.8 = (f32[128,16]{0,1:T(8,128)S(1)}, f32[128,16]{0,1:T(8,128)S(1)}, u32[]{:S(2)}, u32[]{:S(2)}) collective-permute-start(f32[128,16]{0,1:T(8,128)S(1)} %slice_select_fusion.7), channel_id=1, source_target_pairs={{0,8},{1,9},{2,10},{3,11},{4,12},{5,13},{6,14},{7,15},{8,0},{9,1},... | collective-permute-start | bytes 24584 | tf_op jit(solution)/shard_map/ppermute | solution.py:12
  9.5 2.1 convolution_bitcast_fusion
  13.6 1.9 collective-permute-start.1
  16.4 1.5 collective-permute-start.2
  20.0 1.6 collective-permute-done.9
  21.7 22.5 %collective-permute-done.1 = f32[128,2560]{0,1:T(8,128)} collective-permute-done((f32[128,2560]{0,1:T(8,128)}, f32[128,2560]{0,1:T(8,128)}, u32[]{:S(2)}, u32[]{:S(2)}) %collective-permute-start.1) | collective-permute-done | bytes 1310752 | tf_op jit(solution)/shard_map/ppermute | solution.py:12
  44.2 2.5 %multiply_add_fusion.2 = f32[128,16,160]{0,2,1:T(8,128)S(1)} fusion(f32[128,16,160]{0,2,1:T(8,128)} %bitcast.6, f32[256,16,160]{0,2,1:T(8,128)} %copy-done.4, f32[128,16]{0,1:T(8,128)S(1)} %get-tuple-element.22, f32[128,16]{0,1:T(8,128)S(1)} %get-tuple-element.21, pred[]{:T(512)S(6)} %eq.46), kind=kLoop, calls=%fused_computation.19 | loop fusion | flops 1310720 | bytes 5259265 | tf_op jit(solution)/shard_map/add | solution.py:24
  46.6 1.5 slice_select_fusion.2
  48.2 1.7 copy.44
  49.9 1.7 collective-permute-start.3
  51.6 1.5 collective-permute-start.4
  55.3 1.6 collective-permute-done.10
  56.9 8.5 %collective-permute-done.3 = f32[64,2560]{1,0:T(8,128)} collective-permute-done((f32[64,2560]{1,0:T(8,128)S(1)}, f32[64,2560]{1,0:T(8,128)}, u32[]{:S(2)}, u32[]{:S(2)}) %collective-permute-start.3) | collective-permute-done | bytes 655392 | tf_op jit(solution)/shard_map/ppermute | solution.py:12
  65.4 2.6 %copy.45 = f32[64,2560]{0,1:T(8,128)} copy(f32[64,2560]{1,0:T(8,128)} %collective-permute-done.3) | data formatting | bytes 1310720 | tf_op jit(solution)/shard_map/ppermute | solution.py:12
  67.9 2.6 %multiply_add_fusion.1 = f32[64,16,160]{0,2,1:T(8,128)S(1)} fusion(f32[64,16,160]{0,2,1:T(8,128)} %bitcast.64, f32[128,16,160]{0,2,1:T(8,128)} %copy-done.1, f32[64,16]{0,1:T(8,128)S(1)} %get-tuple-element.18, f32[64,16]{0,1:T(8,128)S(1)} %get-tuple-element.17, pred[]{:T(512)S(6)} %eq.45), kind=kLoop, calls=%fused_computation.18 | loop fusion | flops 655360 | bytes 2629633 | tf_op jit(solution)/shard_map/add | solution.py:24
  70.5 1.5 slice_select_fusion.1
  72.0 1.7 copy.46
  75.7 5.5 %collective-permute-done.5 = f32[32,2560]{1,0:T(8,128)S(1)} collective-permute-done((f32[32,2560]{1,0:T(8,128)S(1)}, f32[32,2560]{1,0:T(8,128)S(1)}, u32[]{:S(2)}, u32[]{:S(2)}) %collective-permute-start.5) | collective-permute-done | bytes 327712 | tf_op jit(solution)/shard_map/ppermute | solution.py:12
  81.2 1.5 copy.47
  82.7 2.6 %multiply_add_fusion = f32[32,16,160]{0,2,1:T(8,128)S(1)} fusion(f32[32,16,160]{0,2,1:T(8,128)} %bitcast.63, f32[64,16,160]{0,2,1:T(8,128)} %copy-done.3, f32[32,16]{0,1:T(8,128)S(1)} %get-tuple-element.14, f32[32,16]{0,1:T(8,128)S(1)} %get-tuple-element.13, pred[]{:T(512)S(6)} %eq.44), kind=kLoop, calls=%fused_computation.17 | loop fusion | flops 327680 | bytes 1314817 | tf_op jit(solution)/shard_map/add | solution.py:24
  85.3 1.5 slice_select_fusion
  86.8 1.7 copy.48
  91.4 2.7 %multiply_reduce_fusion.1 = (f32[16]{0:T(128)S(1)}, f32[16,16,160]{0,2,1:T(8,128)S(1)}) fusion(f32[16,16]{0,1:T(8,128)S(1)} %get-tuple-element.9, f32[16,16,160]{0,2,1:T(8,128)} %bitcast.62, f32[16,16]{0,1:T(8,128)S(1)} %get-tuple-element.11, f32[16,16]{0,1:T(8,128)S(1)} %get-tuple-element.10, f32[32,16,160]{0,2,1:T(8,128)} %copy-done.2, pred[]{:T(512)S(6)} %eq.43), kind=kLoop, calls=%fused_computation.15 | loop fusion | flops 368624 | bytes 658497 | tf_op jit(solution)/shard_map/reduce_sum | solution.py:79
  95.5 65.8 %all_to_all.10 = bf16[32,16,2560]{2,1,0:T(8,128)(2,1)S(1)} all-to-all(bf16[32,16,2560]{2,1,0:T(8,128)(2,1)S(1)} %bitcast.58), channel_id=1, replica_groups=mesh['groups'=1,'wide'=32] {'wide'}, dimensions={0} | all-to-all | bytes 5242880 | tf_op jit(solution)/shard_map/all_to_all | solution.py:105
  161.3 1.5 copy-done.7
  162.8 2.5 %convolution_bitcast_fusion.2 = f32[512,512]{0,1:T(8,128)} fusion(bf16[512,2560]{1,0:T(8,128)(2,1)S(1)} %bitcast.67, bf16[512,2560]{1,0:T(8,128)(2,1)S(1)} %copy-done.11), kind=kOutput, calls=%fused_computation.12 | convolution fusion | flops 1342177280 | bytes 6291456 | tf_op jit(solution)/shard_map/dot_general | solution.py:108
  165.3 7.3 %convolution_convert_fusion = bf16[512,2560]{1,0:T(8,128)(2,1)} fusion(bf16[512,2560]{1,0:T(8,128)(2,1)S(1)} %copy-done, bf16[512,2560]{1,0:T(8,128)(2,1)} %bitcast.68, bf16[512,2560]{1,0:T(8,128)(2,1)} %param.16, f32[512,512]{0,1:T(8,128)} %convolution_bitcast_fusion.2), kind=kOutput, calls=%fused_computation.1 | convolution fusion | flops 2687238144 | bytes 11534336 | tf_op jit(solution)/shard_map/dot_general | solution.py:115
  172.6 3.8 %all-to-all-start.1 = ((bf16[32,16,2560]{2,1,0:T(8,128)(2,1)}), bf16[32,16,2560]{2,1,0:T(8,128)(2,1)}, u32[]{:S(2)}, u32[]{:S(2)}) async-start(bf16[32,16,2560]{2,1,0:T(8,128)(2,1)} %bitcast.66), calls=%async_computation.1 | async-start | bytes 5242880 | tf_op jit(solution)/shard_map/all_to_all | solution.py:119
  176.7 1.7 copy.54
  178.4 58.1 %all-to-all-done.1 = bf16[32,16,2560]{2,1,0:T(8,128)(2,1)} async-done(((bf16[32,16,2560]{2,1,0:T(8,128)(2,1)}), bf16[32,16,2560]{2,1,0:T(8,128)(2,1)}, u32[]{:S(2)}, u32[]{:S(2)}) %all-to-all-start.1) | async-done | bytes 2621472 | tf_op jit(solution)/shard_map/all_to_all | solution.py:119
  236.5 3.7 %bitcast_reduce_fusion = bf16[16,16,2560]{2,1,0:T(8,128)(2,1)} fusion(bf16[32,16,2560]{2,1,0:T(8,128)(2,1)} %all-to-all-done.1), kind=kLoop, calls=%fused_computation.3 | loop fusion | flops 655360 | bytes 3932160 | tf_op jit(solution)/shard_map/reduce_sum | solution.py:123
  240.2 3.6 %gather_fusion = bf16[96,2560]{1,0:T(8,128)(2,1)} fusion(bf16[256,2560]{1,0:T(8,128)(2,1)} %bitcast.55, s32[1024]{0:T(1024)S(1)} %pad_clamp_fusion), kind=kCustom, calls=%fused_computation | custom fusion | bytes 983424 | tf_op jit(solution)/shard_map/jit(_take)/gather | solution.py:128
  (78 shorter events, 22.5 us)
Async XLA Ops:
  0.0 165.3 %copy-start = (bf16[512,2560]{1,0:T(8,128)(2,1)S(1)}, bf16[512,2560]{1,0:T(8,128)(2,1)}, u32[]{:S(2)}) copy-start(bf16[512,2560]{1,0:T(8,128)(2,1)} %param.17) | copy-start | bytes 7864324
  3.1 1.4 copy-start.5
  4.9 11.4 %collective-permute-start.8 = (f32[128,16]{0,1:T(8,128)S(1)}, f32[128,16]{0,1:T(8,128)S(1)}, u32[]{:S(2)}, u32[]{:S(2)}) collective-permute-start(f32[128,16]{0,1:T(8,128)S(1)} %slice_select_fusion.7), channel_id=1, source_target_pairs={{0,8},{1,9},{2,10},{3,11},{4,12},{5,13},{6,14},{7,15},{8,0},{9,1},... | collective-permute-start | bytes 24584 | tf_op jit(solution)/shard_map/ppermute | solution.py:12
  8.0 8.2 %collective-permute-start = (f32[128,16]{0,1:T(8,128)S(1)}, f32[128,16]{0,1:T(8,128)S(1)}, u32[]{:S(2)}, u32[]{:S(2)}) collective-permute-start(f32[128,16]{0,1:T(8,128)S(1)} %slice_select_fusion.14), channel_id=1, source_target_pairs={{0,8},{1,9},{2,10},{3,11},{4,12},{5,13},{6,14},{7,15},{8,0},{9,1},... | collective-permute-start | bytes 24584 | tf_op jit(solution)/shard_map/ppermute | solution.py:12
  11.6 2.0 copy-start.4
  11.6 3.9 %copy-start.10 = (s32[16,6]{0,1:T(8,128)S(1)}, s32[16,6]{0,1:T(8,128)}, u32[]{:S(2)}) copy-start(s32[16,6]{0,1:T(8,128)} %param.13) | copy-start | bytes 1156
  13.6 30.6 %collective-permute-start.1 = (f32[128,2560]{0,1:T(8,128)}, f32[128,2560]{0,1:T(8,128)}, u32[]{:S(2)}, u32[]{:S(2)}) collective-permute-start(f32[128,2560]{0,1:T(8,128)} %bitcast.5), channel_id=1, source_target_pairs={{0,8},{1,9},{2,10},{3,11},{4,12},{5,13},{6,14},{7,15},{8,0},{9,1},... | collective-permute-start | bytes 3932168 | tf_op jit(solution)/shard_map/ppermute | solution.py:12
  16.4 3.7 %collective-permute-start.2 = (f32[64,16]{0,1:T(8,128)S(1)}, f32[64,16]{0,1:T(8,128)S(1)}, u32[]{:S(2)}, u32[]{:S(2)}) collective-permute-start(f32[64,16]{0,1:T(8,128)S(1)} %slice_select_fusion.12), channel_id=1, source_target_pairs={{0,4},{1,5},{2,6},{3,7},{4,0},{5,1},{6,2},{7,3},{8,12},{9,13},{10,... | collective-permute-start | bytes 12296 | tf_op jit(solution)/shard_map/ppermute | solution.py:12
  18.0 3.7 %collective-permute-start.9 = (f32[64,16]{0,1:T(8,128)S(1)}, f32[64,16]{0,1:T(8,128)S(1)}, u32[]{:S(2)}, u32[]{:S(2)}) collective-permute-start(f32[64,16]{0,1:T(8,128)S(1)} %slice_select_fusion.6), channel_id=1, source_target_pairs={{0,4},{1,5},{2,6},{3,7},{4,0},{5,1},{6,2},{7,3},{8,12},{9,13},{10,... | collective-permute-start | bytes 12296 | tf_op jit(solution)/shard_map/ppermute | solution.py:12
  46.6 1.5 copy-start.1
  49.9 15.5 %collective-permute-start.3 = (f32[64,2560]{1,0:T(8,128)S(1)}, f32[64,2560]{1,0:T(8,128)}, u32[]{:S(2)}, u32[]{:S(2)}) collective-permute-start(f32[64,2560]{1,0:T(8,128)S(1)} %copy.44), channel_id=1, source_target_pairs={{0,4},{1,5},{2,6},{3,7},{4,0},{5,1},{6,2},{7,3},{8,12},{9,13},{10,... | collective-permute-start | bytes 1966088 | tf_op jit(solution)/shard_map/ppermute | solution.py:12
  51.6 3.7 %collective-permute-start.4 = (f32[32,16]{0,1:T(8,128)S(1)}, f32[32,16]{0,1:T(8,128)S(1)}, u32[]{:S(2)}, u32[]{:S(2)}) collective-permute-start(f32[32,16]{0,1:T(8,128)S(1)} %slice_select_fusion.10), channel_id=1, source_target_pairs={{0,2},{1,3},{2,0},{3,1},{4,6},{5,7},{6,4},{7,5},{8,10},{9,11},{10,... | collective-permute-start | bytes 6152 | tf_op jit(solution)/shard_map/ppermute | solution.py:12
  53.2 3.7 %collective-permute-start.10 = (f32[32,16]{0,1:T(8,128)S(1)}, f32[32,16]{0,1:T(8,128)S(1)}, u32[]{:S(2)}, u32[]{:S(2)}) collective-permute-start(f32[32,16]{0,1:T(8,128)S(1)} %slice_select_fusion.5), channel_id=1, source_target_pairs={{0,2},{1,3},{2,0},{3,1},{4,6},{5,7},{6,4},{7,5},{8,10},{9,11},{10,... | collective-permute-start | bytes 6152 | tf_op jit(solution)/shard_map/ppermute | solution.py:12
  70.5 1.5 copy-start.3
  73.7 7.5 %collective-permute-start.5 = (f32[32,2560]{1,0:T(8,128)S(1)}, f32[32,2560]{1,0:T(8,128)S(1)}, u32[]{:S(2)}, u32[]{:S(2)}) collective-permute-start(f32[32,2560]{1,0:T(8,128)S(1)} %copy.46), channel_id=1, source_target_pairs={{0,2},{1,3},{2,0},{3,1},{4,6},{5,7},{6,4},{7,5},{8,10},{9,11},{10,... | collective-permute-start | bytes 983048 | tf_op jit(solution)/shard_map/ppermute | solution.py:12
  75.1 13.4 %collective-permute-start.6 = (f32[16,16]{0,1:T(8,128)S(1)}, f32[16,16]{0,1:T(8,128)S(1)}, u32[]{:S(2)}, u32[]{:S(2)}) collective-permute-start(f32[16,16]{0,1:T(8,128)S(1)} %slice_select_fusion.8), channel_id=1, source_target_pairs={{0,1},{1,0},{2,3},{3,2},{4,5},{5,4},{6,7},{7,6},{8,9},{9,8},{10,11... | collective-permute-start | bytes 3080 | tf_op jit(solution)/shard_map/ppermute | solution.py:12
  75.2 13.3 %collective-permute-start.11 = (f32[16,16]{0,1:T(8,128)S(1)}, f32[16,16]{0,1:T(8,128)S(1)}, u32[]{:S(2)}, u32[]{:S(2)}) collective-permute-start(f32[16,16]{0,1:T(8,128)S(1)} %slice_select_fusion.4), channel_id=1, source_target_pairs={{0,1},{1,0},{2,3},{3,2},{4,5},{5,4},{6,7},{7,6},{8,9},{9,8},{10,11... | collective-permute-start | bytes 3080 | tf_op jit(solution)/shard_map/ppermute | solution.py:12
  85.3 1.5 copy-start.2
  88.5 1.4 collective-permute-start.7
  91.4 2.7 %copy-start.9 = (f32[2560]{0:T(1024)S(1)}, f32[2560]{0:T(1024)}, u32[]{:S(2)}) copy-start(f32[2560]{0:T(1024)} %param.12) | copy-start | bytes 30724
  94.1 1.1 copy-start.6
  95.5 67.3 %copy-start.11 = (bf16[512,2560]{1,0:T(8,128)(2,1)S(1)}, bf16[512,2560]{1,0:T(8,128)(2,1)}, u32[]{:S(2)}) copy-start(bf16[512,2560]{1,0:T(8,128)(2,1)} %param.15) | copy-start | bytes 7864324
  161.2 1.5 copy-start.7
  172.6 3.8 %copy-start.8 = (s32[16,6]{0,1:T(8,128)S(1)}, s32[16,6]{0,1:T(8,128)}, u32[]{:S(2)}) copy-start(s32[16,6]{0,1:T(8,128)} %param.14) | copy-start | bytes 1156
  172.6 63.9 %all-to-all-start.1 = ((bf16[32,16,2560]{2,1,0:T(8,128)(2,1)}), bf16[32,16,2560]{2,1,0:T(8,128)(2,1)}, u32[]{:S(2)}, u32[]{:S(2)}) async-start(bf16[32,16,2560]{2,1,0:T(8,128)(2,1)} %bitcast.66), calls=%async_computation.1 | async-start | bytes 5242880 | tf_op jit(solution)/shard_map/all_to_all | solution.py:119
where the time goes:
time: 247 us; the launch traced here: 246 us
  waiting for transfers between devices  102 us (41%)
  blocking collectives  65.8 us (27%)
  local copies, waits for them, and re-layouts  25.8 us (10%)
  other arithmetic  22.6 us (9%)
  starting transfers between devices  16.6 us (7%)
  matrix products  13.2 us (5%)
    all_to_all x1, blocking collectives, on_device(): lax.all_to_all(sent_rows, 'wide', split_axis=0, concat_axis=0, tiled=True)  65.8 us
    all_to_all x1, waiting for transfers between devices, on_device(): lax.all_to_all(partial_value.astype(jnp.bfloat16), 'wide', split_axis=0,...  58.1 us
    ppermute x12, waiting for transfers between devices, partner(): return lax.ppermute(value, axis, pairs)  43.8 us
    ppermute x12, starting transfers between devices, partner(): return lax.ppermute(value, axis, pairs)  12.8 us
    unnamed x28, local copies, waits for them, and re-layouts  7.97 us
    add x3, other arithmetic, merge_partials(): summed + sum_second.reshape(row_count, head_count, -1) * factor_second[:,...  7.6 us
    dot_general x1, matrix products, on_device(): lax.dot_general(hidden, w_down, (((0,), (0,)), ((), ())), preferred_eleme...  7.29 us
    select_n x4, other arithmetic, on_device(): sent_sum = jnp.where(upper_half, summed[:half_rows], summed[half_rows:])  5.86 us
  transfers between devices with their start and end apart: 13, of which 9 were waited for; matrix products, arithmetic and copies ran while one was open for 6% of the time, Pallas kernels for 0%

commit v1 on v0

--- a/solution.py
+++ b/solution.py
@@ -10,6 +10,21 @@
     mask = 2**stride
     pairs = [(source, source ^ mask) for source in range(lax.axis_size(axis))]
     return lax.ppermute(value, axis, pairs)
+
+
+def stage_orders(devices):
+    bits = list(reversed(range(1, devices.bit_length() - 1)))
+    other = bits[:-2] + bits[-2:][::-1]
+    other = other[:2][::-1] + other[2:] if len(other) > 3 else other
+    return (bits, other)
+
+
+def exchange(value, orders, stage):
+    pairs = [
+        (source, source ^ (1 << orders[source % 2][stage]))
+        for source in range(lax.axis_size("wide"))
+    ]
+    return lax.ppermute(value, "wide", pairs)
 
 
 def merge_partials(first_part, second_part, head_count):
@@ -80,59 +95,48 @@
         * norm_gain
     ).astype(jnp.bfloat16)
     experts = devices // 2
-    capacity = 32 * row_count // devices
-    flat_routes = route_experts.reshape(-1)
-    onehot = (flat_routes[:, None] == jnp.arange(experts, dtype=jnp.int32)[None, :]).astype(
-        jnp.int32
+    lane_pad = -experts % 128
+    score_table = jnp.sum(
+        jnp.where(
+            route_experts[:, :, None] == jnp.arange(experts, dtype=jnp.int32)[None, None, :],
+            route_weights[:, :, None],
+            0,
+        ),
+        axis=1,
+    ).astype(jnp.bfloat16)
+    block = jnp.concatenate(
+        [normed, score_table, jnp.zeros((row_count, lane_pad), jnp.bfloat16)], axis=1
     )
-    earlier = jnp.cumsum(onehot, axis=0) - onehot
-    slot_index = jnp.sum(earlier * onehot, axis=1)
-    position = flat_routes * capacity + slot_index
-    placing = jnp.any(
-        position.reshape(row_count, top_k)[:, :, None]
-        == jnp.arange(experts * capacity, dtype=jnp.int32)[None, None, :],
-        axis=1,
+    orders = stage_orders(devices)
+    for stage in range(len(orders[0])):
+        block = jnp.concatenate([block, exchange(block, orders, stage)], axis=0)
+    block = jnp.concatenate([block, partner(block, "wide", 0)], axis=0)
+    rows_in = block[:, :model_width]
+    score_rows = block[:, model_width : model_width + experts].astype(jnp.float32)
+    own_expert = jnp.arange(experts, dtype=jnp.int32)[None, :] == device_index // 2
+    share = jnp.sum(jnp.where(own_expert, score_rows, 0.0), axis=1, keepdims=True) / jnp.sum(
+        score_rows, axis=1, keepdims=True
     )
-    buffer = lax.dot_general(
-        placing.astype(jnp.bfloat16),
-        normed,
-        (((0,), (0,)), ((), ())),
-        preferred_element_type=jnp.float32,
-    ).astype(jnp.bfloat16)
-    sent_rows = jnp.broadcast_to(
-        buffer.reshape(experts, 1, capacity, model_width), (experts, 2, capacity, model_width)
-    ).reshape(devices, capacity, model_width)
-    received = lax.all_to_all(sent_rows, "wide", split_axis=0, concat_axis=0, tiled=True)
-    sources, item_count, row_width = received.shape
-    flat_rows = received.reshape(sources * item_count, row_width)
     gate_part = lax.dot_general(
-        w_gate, flat_rows, (((1,), (1,)), ((), ())), preferred_element_type=jnp.float32
+        rows_in, w_gate, (((1,), (1,)), ((), ())), preferred_element_type=jnp.float32
     )
     up_part = lax.dot_general(
-        w_up, flat_rows, (((1,), (1,)), ((), ())), preferred_element_type=jnp.float32
+        rows_in, w_up, (((1,), (1,)), ((), ())), preferred_element_type=jnp.float32
     )
-    hidden = (jax.nn.silu(gate_part) * up_part).astype(jnp.bfloat16)
+    hidden = (jax.nn.silu(gate_part) * up_part * share).astype(jnp.bfloat16)
     partial_value = lax.dot_general(
-        hidden, w_down, (((0,), (0,)), ((), ())), preferred_element_type=jnp.float32
+        hidden, w_down, (((1,), (0,)), ((), ())), preferred_element_type=jnp.float32
     )
-    partial_value = partial_value.reshape(sources, item_count, row_width)
-    returned = lax.all_to_all(
-        partial_value.astype(jnp.bfloat16), "wide", split_axis=0, concat_axis=0, tiled=True
-    ).astype(partial_value.dtype)
-    outputs = (
-        jnp.sum(returned.reshape(experts, 2, -1, model_width), axis=1)
-        .astype(jnp.bfloat16)
-        .reshape(-1, model_width)
-    )
-    picked = (
-        jnp.take(outputs, position, axis=0)
-        .reshape(row_count, top_k, model_width)
-        .astype(jnp.float32)
-    )
-    scores_int = route_weights.astype(jnp.float32)
-    gate_share = scores_int / jnp.sum(scores_int, axis=1, keepdims=True)
-    mixed_rows = residual + jnp.sum(picked * gate_share[:, :, None], axis=1)
-    return mixed_rows.astype(jnp.bfloat16)
+    half_rows = partial_value.shape[0] // 2
+    total = partial_value[:half_rows] + partner(
+        partial_value[half_rows:].astype(jnp.bfloat16), "wide", 0
+    ).astype(jnp.float32)
+    for stage in reversed(range(len(orders[0]))):
+        half_rows = total.shape[0] // 2
+        total = total[:half_rows] + exchange(
+            total[half_rows:].astype(jnp.bfloat16), orders, stage
+        ).astype(jnp.float32)
+    return (residual + total).astype(jnp.bfloat16)
 
 
 def solution(mesh):

time: 247 us -> 183 us (0.74)
  blocking collectives: 65.8 us -> 0 us
  starting transfers between devices: 16.6 us -> 25.2 us
  local copies, waits for them, and re-layouts: 25.8 us -> 22.5 us
    all_to_all x1 -> x0, blocking collectives: 65.8 us -> none  [on_device(): lax.all_to_all(sent_rows, 'wide', split_axis=0, concat_axis=0, tiled=True)]
    all_to_all x1 -> x0, waiting for transfers between devices: 58.1 us -> none  [on_device(): lax.all_to_all(partial_value.astype(jnp.bfloat16), 'wide', split_axis=0,...]
    ppermute x0 -> x8, waiting for transfers between devices: none -> 45.9 us  [exchange(): return lax.ppermute(value, 'wide', pairs)]
    ppermute x0 -> x8, starting transfers between devices: none -> 13.2 us  [exchange(): return lax.ppermute(value, 'wide', pairs)]
    ppermute x12 -> x14, waiting for transfers between devices: 43.8 us -> 54 us  [partner(): return lax.ppermute(value, axis, pairs)]
    gather x2 -> x0, local copies, waits for them, and re-layouts: 4.82 us -> none  [on_device(): jnp.take(outputs, position, axis=0).reshape(row_count, top_k, model_width)]
    reduce_sum x4 -> x2, other arithmetic: 4.42 us -> 0.24 us  [the longest x1 0.15 us: on_device(): jnp.sum(score_rows, axis=1, keepdims=True)]
    all_to_all x1 -> x0, starting transfers between devices: 3.83 us -> none  [on_device(): lax.all_to_all(partial_value.astype(jnp.bfloat16), 'wide', split_axis=0,...]
  transfers between devices with their start and end apart: 13 -> 22, of which waited for: 9 -> 19; matrix products, arithmetic and copies ran while one was open for 6% -> 5% of each run, Pallas kernels for 0% -> 0%
where the time goes in v1:
time: 183 us
  waiting for transfers between devices  99.9 us (55%)
  starting transfers between devices  25.2 us (14%)
  local copies, waits for them, and re-layouts  22.5 us (12%)
  other arithmetic  21.7 us (12%)
  matrix products  13 us (7%)
    ppermute x14, waiting for transfers between devices, partner(): return lax.ppermute(value, axis, pairs)  54 us
    ppermute x8, waiting for transfers between devices, exchange(): return lax.ppermute(value, 'wide', pairs)  45.9 us
    ppermute x8, starting transfers between devices, exchange(): return lax.ppermute(value, 'wide', pairs)  13.2 us
    ppermute x14, starting transfers between devices, partner(): return lax.ppermute(value, axis, pairs)  12 us
    dot_general x1, matrix products, on_device(): lax.dot_general(hidden, w_down, (((1,), (0,)), ((), ())), preferred_eleme...  8.2 us
    unnamed x27, local copies, waits for them, and re-layouts  7.86 us
    add x3, other arithmetic, merge_partials(): summed + sum_second.reshape(row_count, head_count, -1) * factor_second[:,...  7.61 us
    select_n x4, other arithmetic, on_device(): sent_sum = jnp.where(upper_half, summed[:half_rows], summed[half_rows:])  5.79 us
  transfers between devices with their start and end apart: 22, of which 19 were waited for; matrix products, arithmetic and copies ran while one was open for 5% of the time, Pallas kernels for 0%

profile of v1, /device:TPU:0, one launch (start us, length us, event | category | flops | bytes accessed | tf_op | source)
XLA Modules:
  0.0 182.6 jit_solution(73664903556316281)
XLA Ops:
  0.0 2.0 %copy.38 = bf16[128,1152]{0,1:T(8,128)(2,1)} copy(bf16[128,1152]{1,0:T(8,128)(2,1)} %param.10) | data formatting | bytes 589824 | tf_op args[1]
  2.0 2.2 %copy.39 = bf16[256,1152]{0,1:T(8,128)(2,1)} copy(bf16[256,1152]{1,0:T(8,128)(2,1)} %param.9) | data formatting | bytes 1179648 | tf_op args[0]
  9.7 3.1 %collective-permute-start.1 = (f32[128,2560]{0,1:T(8,128)}, f32[128,2560]{0,1:T(8,128)}, u32[]{:S(2)}, u32[]{:S(2)}) collective-permute-start(f32[128,2560]{0,1:T(8,128)} %bitcast.5), channel_id=1, source_target_pairs={{0,8},{1,9},{2,10},{3,11},{4,12},{5,13},{6,14},{7,15},{8,0},{9,1},... | collective-permute-start | bytes 3932168 | tf_op jit(solution)/shard_map/ppermute | solution.py:12
  13.2 2.0 %collective-permute-start = (f32[128,16]{0,1:T(8,128)S(1)}, f32[128,16]{0,1:T(8,128)S(1)}, u32[]{:S(2)}, u32[]{:S(2)}) collective-permute-start(f32[128,16]{0,1:T(8,128)S(1)} %slice_select_fusion.14), channel_id=1, source_target_pairs={{0,8},{1,9},{2,10},{3,11},{4,12},{5,13},{6,14},{7,15},{8,0},{9,1},... | collective-permute-start | bytes 24584 | tf_op jit(solution)/shard_map/ppermute | solution.py:12
  15.2 26.8 %collective-permute-done.8 = f32[128,16]{0,1:T(8,128)S(1)} collective-permute-done((f32[128,16]{0,1:T(8,128)S(1)}, f32[128,16]{0,1:T(8,128)S(1)}, u32[]{:S(2)}, u32[]{:S(2)}) %collective-permute-start.8) | collective-permute-done | bytes 8224 | tf_op jit(solution)/shard_map/ppermute | solution.py:12
  45.8 1.8 collective-permute-done.2
  47.7 2.5 %multiply_add_fusion.2 = f32[128,16,160]{0,2,1:T(8,128)S(1)} fusion(f32[128,16,160]{0,2,1:T(8,128)} %bitcast.6, f32[256,16,160]{0,2,1:T(8,128)} %copy-done.4, f32[128,16]{0,1:T(8,128)S(1)} %get-tuple-element.22, f32[128,16]{0,1:T(8,128)S(1)} %get-tuple-element.21, pred[]{:T(512)S(6)} %eq.44), kind=kLoop, calls=%fused_computation.18 | loop fusion | flops 1310720 | bytes 5259265 | tf_op jit(solution)/shard_map/add | solution.py:39
  51.7 1.7 copy.42
  57.5 1.7 collective-permute-done.4
  59.4 8.5 %collective-permute-done.3 = f32[64,2560]{1,0:T(8,128)} collective-permute-done((f32[64,2560]{1,0:T(8,128)S(1)}, f32[64,2560]{1,0:T(8,128)}, u32[]{:S(2)}, u32[]{:S(2)}) %collective-permute-start.3) | collective-permute-done | bytes 655392 | tf_op jit(solution)/shard_map/ppermute | solution.py:12
  67.9 2.5 %copy.43 = f32[64,2560]{0,1:T(8,128)} copy(f32[64,2560]{1,0:T(8,128)} %collective-permute-done.3) | data formatting | bytes 1310720 | tf_op jit(solution)/shard_map/ppermute | solution.py:12
  70.4 2.6 %multiply_add_fusion.1 = f32[64,16,160]{0,2,1:T(8,128)S(1)} fusion(f32[64,16,160]{0,2,1:T(8,128)} %bitcast.36, f32[128,16,160]{0,2,1:T(8,128)} %copy-done.1, f32[64,16]{0,1:T(8,128)S(1)} %get-tuple-element.18, f32[64,16]{0,1:T(8,128)S(1)} %get-tuple-element.17, pred[]{:T(512)S(6)} %eq.43), kind=kLoop, calls=%fused_computation.17 | loop fusion | flops 655360 | bytes 2629633 | tf_op jit(solution)/shard_map/add | solution.py:39
  78.4 4.9 %collective-permute-done.5 = f32[32,2560]{1,0:T(8,128)S(1)} collective-permute-done((f32[32,2560]{1,0:T(8,128)S(1)}, f32[32,2560]{1,0:T(8,128)S(1)}, u32[]{:S(2)}, u32[]{:S(2)}) %collective-permute-start.5) | collective-permute-done | bytes 327712 | tf_op jit(solution)/shard_map/ppermute | solution.py:12
  84.8 2.6 %multiply_add_fusion = f32[32,16,160]{0,2,1:T(8,128)S(1)} fusion(f32[32,16,160]{0,2,1:T(8,128)} %bitcast.35, f32[64,16,160]{0,2,1:T(8,128)} %copy-done.3, f32[32,16]{0,1:T(8,128)S(1)} %get-tuple-element.14, f32[32,16]{0,1:T(8,128)S(1)} %get-tuple-element.13, pred[]{:T(512)S(6)} %eq.42), kind=kLoop, calls=%fused_computation.16 | loop fusion | flops 327680 | bytes 1314817 | tf_op jit(solution)/shard_map/add | solution.py:39
  93.4 3.7 %multiply_reduce_fusion = (f32[16]{0:T(128)S(1)}, f32[16,16,160]{0,2,1:T(8,128)}) fusion(f32[16,16]{0,1:T(8,128)S(1)} %get-tuple-element.9, f32[16,16,160]{0,2,1:T(8,128)} %bitcast.33, f32[16,16]{0,1:T(8,128)S(1)} %get-tuple-element.11, f32[16,16]{0,1:T(8,128)S(1)} %get-tuple-element.10, f32[32,16,160]{0,2,1:T(8,128)} %copy-done.2, pred[]{:T(512)S(6)} %eq.41), kind=kLoop, calls=%fused_computation.14 | loop fusion | flops 368624 | bytes 658497 | tf_op jit(solution)/shard_map/reduce_sum | solution.py:94
  99.0 2.6 %collective-permute-start.12 = (bf16[16,2688]{1,0:T(8,128)(2,1)S(1)}, bf16[16,2688]{1,0:T(8,128)(2,1)S(1)}, u32[]{:S(2)}, u32[]{:S(2)}) collective-permute-start(bf16[16,2688]{1,0:T(8,128)(2,1)S(1)} %concatenate.22), channel_id=1, source_target_pairs={{0,16},{1,9},{2,18},{3,11},{4,20},{5,13},{6,22},{7,15},{8,24},{9,1... | collective-permute-start | bytes 258056 | tf_op jit(solution)/shard_map/ppermute | solution.py:27
  101.6 2.8 %collective-permute-done.12 = bf16[16,2688]{1,0:T(8,128)(2,1)S(1)} collective-permute-done((bf16[16,2688]{1,0:T(8,128)(2,1)S(1)}, bf16[16,2688]{1,0:T(8,128)(2,1)S(1)}, u32[]{:S(2)}, u32[]{:S(2)}) %collective-permute-start.12) | collective-permute-done | bytes 86048 | tf_op jit(solution)/shard_map/ppermute | solution.py:27
  104.4 1.9 %collective-permute-start.13 = (bf16[32,2688]{1,0:T(8,128)(2,1)S(1)}, bf16[32,2688]{1,0:T(8,128)(2,1)S(1)}, u32[]{:S(2)}, u32[]{:S(2)}) collective-permute-start(bf16[32,2688]{1,0:T(8,128)(2,1)S(1)} %pad_maximum_fusion.2), channel_id=1, source_target_pairs={{0,8},{1,17},{2,10},{3,19},{4,12},{5,21},{6,14},{7,23},{8,0},{9,25... | collective-permute-start | bytes 516104 | tf_op jit(solution)/shard_map/ppermute | solution.py:27
  106.3 4.5 %collective-permute-done.13 = bf16[32,2688]{1,0:T(8,128)(2,1)S(1)} collective-permute-done((bf16[32,2688]{1,0:T(8,128)(2,1)S(1)}, bf16[32,2688]{1,0:T(8,128)(2,1)S(1)}, u32[]{:S(2)}, u32[]{:S(2)}) %collective-permute-start.13) | collective-permute-done | bytes 172064 | tf_op jit(solution)/shard_map/ppermute | solution.py:27
  111.6 6.6 %collective-permute-done.14 = bf16[64,2688]{1,0:T(8,128)(2,1)S(1)} collective-permute-done((bf16[64,2688]{1,0:T(8,128)(2,1)S(1)}, bf16[64,2688]{1,0:T(8,128)(2,1)S(1)}, u32[]{:S(2)}, u32[]{:S(2)}) %collective-permute-start.14) | collective-permute-done | bytes 344096 | tf_op jit(solution)/shard_map/ppermute | solution.py:27
  119.9 9.4 %collective-permute-done.15 = bf16[128,2688]{1,0:T(8,128)(2,1)S(1)} collective-permute-done((bf16[128,2688]{1,0:T(8,128)(2,1)S(1)}, bf16[128,2688]{1,0:T(8,128)(2,1)S(1)}, u32[]{:S(2)}, u32[]{:S(2)}) %collective-permute-start.15) | collective-permute-done | bytes 688160 | tf_op jit(solution)/shard_map/ppermute | solution.py:27
  129.5 3.1 %collective-permute-done.16 = bf16[256,2688]{1,0:T(8,128)(2,1)S(1)} collective-permute-done((bf16[256,2688]{1,0:T(8,128)(2,1)S(1)}, bf16[256,2688]{1,0:T(8,128)(2,1)S(1)}, u32[]{:S(2)}, u32[]{:S(2)}) %collective-permute-start.16) | collective-permute-done | bytes 1376288 | tf_op jit(solution)/shard_map/ppermute | solution.py:12
  134.3 2.6 %fusion = f32[512,512]{1,0:T(8,128)} fusion(bf16[512,2560]{1,0:T(8,128)(2,1)S(1)} %copy-done.9, bf16[512,2688]{1,0:T(8,128)(2,1)S(1)} %constant_dynamic-update-slice_fusion.5), kind=kOutput, calls=%fused_computation.2 | convolution fusion | flops 1342177280 | bytes 6291456 | tf_op jit(solution)/shard_map/dot_general | solution.py:123
  137.1 8.2 %fusion.11 = f32[512,2560]{1,0:T(8,128)} fusion(bf16[512,2560]{1,0:T(8,128)(2,1)S(1)} %copy-done, f32[512,512]{1,0:T(8,128)} %fusion, bf16[512,2560]{1,0:T(8,128)(2,1)} %param.15, bf16[512,2688]{1,0:T(8,128)(2,1)} %copy-done.5, f32[512]{0:T(512)S(1)} %div.60), kind=kOutput, calls=%fused_computation.30 | convolution fusion | flops 2686189568 | bytes 14157824 | tf_op jit(solution)/shard_map/dot_general | solution.py:127
  145.3 1.9 %slice.325 = bf16[256,2560]{1,0:T(8,128)(2,1)S(1)} slice(f32[512,2560]{1,0:T(8,128)} %fusion.11), slice={[256:512], [0:2560]} | slice | bytes 2621440 | tf_op jit(solution)/shard_map/slice | solution.py:132
  147.4 2.9 %collective-permute-done.17 = bf16[256,2560]{1,0:T(8,128)(2,1)S(1)} collective-permute-done((bf16[256,2560]{1,0:T(8,128)(2,1)S(1)}, bf16[256,2560]{1,0:T(8,128)(2,1)S(1)}, u32[]{:S(2)}, u32[]{:S(2)}) %collective-permute-start.17) | collective-permute-done | bytes 1310752 | tf_op jit(solution)/shard_map/ppermute | solution.py:12
  150.3 2.1 %slice_add_fusion = f32[256,2560]{1,0:T(8,128)S(1)} fusion(f32[512,2560]{1,0:T(8,128)} %fusion.11, bf16[256,2560]{1,0:T(8,128)(2,1)S(1)} %collective-permute-done.17), kind=kLoop, calls=%fused_computation.1 | loop fusion | flops 1310720 | bytes 6553600 | tf_op jit(solution)/shard_map/add | solution.py:131
  154.0 9.1 %collective-permute-done.18 = bf16[128,2560]{1,0:T(8,128)(2,1)S(1)} collective-permute-done((bf16[128,2560]{1,0:T(8,128)(2,1)S(1)}, bf16[128,2560]{1,0:T(8,128)(2,1)S(1)}, u32[]{:S(2)}, u32[]{:S(2)}) %collective-permute-start.18) | collective-permute-done | bytes 655392 | tf_op jit(solution)/shard_map/ppermute | solution.py:27
  164.0 6.4 %collective-permute-done.19 = bf16[64,2560]{1,0:T(8,128)(2,1)S(1)} collective-permute-done((bf16[64,2560]{1,0:T(8,128)(2,1)S(1)}, bf16[64,2560]{1,0:T(8,128)(2,1)S(1)}, u32[]{:S(2)}, u32[]{:S(2)}) %collective-permute-start.19) | collective-permute-done | bytes 327712 | tf_op jit(solution)/shard_map/ppermute | solution.py:27
  171.6 4.7 %collective-permute-done.20 = bf16[32,2560]{1,0:T(8,128)(2,1)S(1)} collective-permute-done((bf16[32,2560]{1,0:T(8,128)(2,1)S(1)}, bf16[32,2560]{1,0:T(8,128)(2,1)S(1)}, u32[]{:S(2)}, u32[]{:S(2)}) %collective-permute-start.20) | collective-permute-done | bytes 163872 | tf_op jit(solution)/shard_map/ppermute | solution.py:27
  176.3 3.3 %collective-permute-start.21 = (bf16[16,2560]{1,0:T(8,128)(2,1)S(1)}, bf16[16,2560]{1,0:T(8,128)(2,1)S(1)}, u32[]{:S(2)}, u32[]{:S(2)}) collective-permute-start(bf16[16,2560]{1,0:T(8,128)(2,1)S(1)} %slice.329), channel_id=1, source_target_pairs={{0,16},{1,9},{2,18},{3,11},{4,20},{5,13},{6,22},{7,15},{8,24},{9,1... | collective-permute-start | bytes 245768 | tf_op jit(solution)/shard_map/ppermute | solution.py:27
  179.6 2.4 %collective-permute-done.21 = bf16[16,2560]{1,0:T(8,128)(2,1)S(1)} collective-permute-done((bf16[16,2560]{1,0:T(8,128)(2,1)S(1)}, bf16[16,2560]{1,0:T(8,128)(2,1)S(1)}, u32[]{:S(2)}, u32[]{:S(2)}) %collective-permute-start.21) | collective-permute-done | bytes 81952 | tf_op jit(solution)/shard_map/ppermute | solution.py:27
  (95 shorter events, 39.5 us)
Async XLA Ops:
  0.0 137.1 %copy-start = (bf16[512,2560]{1,0:T(8,128)(2,1)S(1)}, bf16[512,2560]{1,0:T(8,128)(2,1)}, u32[]{:S(2)}) copy-start(bf16[512,2560]{1,0:T(8,128)(2,1)} %param.17) | copy-start | bytes 7864324
  7.8 1.9 %copy-start.4 = (f32[256,16,160]{0,2,1:T(8,128)}, f32[256,16,160]{0,2,1:T(8,128)S(1)}, u32[]{:S(2)}) copy-start(f32[256,16,160]{0,2,1:T(8,128)S(1)} %convolution_bitcast_fusion) | copy-start | bytes 7864324
  9.7 38.0 %collective-permute-start.1 = (f32[128,2560]{0,1:T(8,128)}, f32[128,2560]{0,1:T(8,128)}, u32[]{:S(2)}, u32[]{:S(2)}) collective-permute-start(f32[128,2560]{0,1:T(8,128)} %bitcast.5), channel_id=1, source_target_pairs={{0,8},{1,9},{2,10},{3,11},{4,12},{5,13},{6,14},{7,15},{8,0},{9,1},... | collective-permute-start | bytes 3932168 | tf_op jit(solution)/shard_map/ppermute | solution.py:12
  13.1 28.9 %collective-permute-start.8 = (f32[128,16]{0,1:T(8,128)S(1)}, f32[128,16]{0,1:T(8,128)S(1)}, u32[]{:S(2)}, u32[]{:S(2)}) collective-permute-start(f32[128,16]{0,1:T(8,128)S(1)} %slice_select_fusion.7), channel_id=1, source_target_pairs={{0,8},{1,9},{2,10},{3,11},{4,12},{5,13},{6,14},{7,15},{8,0},{9,1},... | collective-permute-start | bytes 24584 | tf_op jit(solution)/shard_map/ppermute | solution.py:12
  13.2 28.9 %collective-permute-start = (f32[128,16]{0,1:T(8,128)S(1)}, f32[128,16]{0,1:T(8,128)S(1)}, u32[]{:S(2)}, u32[]{:S(2)}) collective-permute-start(f32[128,16]{0,1:T(8,128)S(1)} %slice_select_fusion.14), channel_id=1, source_target_pairs={{0,8},{1,9},{2,10},{3,11},{4,12},{5,13},{6,14},{7,15},{8,0},{9,1},... | collective-permute-start | bytes 24584 | tf_op jit(solution)/shard_map/ppermute | solution.py:12
  42.2 3.7 %collective-permute-start.9 = (f32[64,16]{0,1:T(8,128)S(1)}, f32[64,16]{0,1:T(8,128)S(1)}, u32[]{:S(2)}, u32[]{:S(2)}) collective-permute-start(f32[64,16]{0,1:T(8,128)S(1)} %slice_select_fusion.6), channel_id=1, source_target_pairs={{0,4},{1,5},{2,6},{3,7},{4,0},{5,1},{6,2},{7,3},{8,12},{9,13},{10,... | collective-permute-start | bytes 12296 | tf_op jit(solution)/shard_map/ppermute | solution.py:12
  43.9 3.7 %collective-permute-start.2 = (f32[64,16]{0,1:T(8,128)S(1)}, f32[64,16]{0,1:T(8,128)S(1)}, u32[]{:S(2)}, u32[]{:S(2)}) collective-permute-start(f32[64,16]{0,1:T(8,128)S(1)} %slice_select_fusion.12), channel_id=1, source_target_pairs={{0,4},{1,5},{2,6},{3,7},{4,0},{5,1},{6,2},{7,3},{8,12},{9,13},{10,... | collective-permute-start | bytes 12296 | tf_op jit(solution)/shard_map/ppermute | solution.py:12
  50.2 1.5 copy-start.1
  51.7 4.3 %copy-start.7 = (s32[16,6]{0,1:T(8,128)S(1)}, s32[16,6]{0,1:T(8,128)}, u32[]{:S(2)}) copy-start(s32[16,6]{0,1:T(8,128)} %param.14) | copy-start | bytes 1156
  51.7 4.3 %copy-start.8 = (s32[16,6]{0,1:T(8,128)S(1)}, s32[16,6]{0,1:T(8,128)}, u32[]{:S(2)}) copy-start(s32[16,6]{0,1:T(8,128)} %param.13) | copy-start | bytes 1156
  53.4 14.5 %collective-permute-start.3 = (f32[64,2560]{1,0:T(8,128)S(1)}, f32[64,2560]{1,0:T(8,128)}, u32[]{:S(2)}, u32[]{:S(2)}) collective-permute-start(f32[64,2560]{1,0:T(8,128)S(1)} %copy.42), channel_id=1, source_target_pairs={{0,4},{1,5},{2,6},{3,7},{4,0},{5,1},{6,2},{7,3},{8,12},{9,13},{10,... | collective-permute-start | bytes 1966088 | tf_op jit(solution)/shard_map/ppermute | solution.py:12
  53.9 3.7 %collective-permute-start.10 = (f32[32,16]{0,1:T(8,128)S(1)}, f32[32,16]{0,1:T(8,128)S(1)}, u32[]{:S(2)}, u32[]{:S(2)}) collective-permute-start(f32[32,16]{0,1:T(8,128)S(1)} %slice_select_fusion.5), channel_id=1, source_target_pairs={{0,2},{1,3},{2,0},{3,1},{4,6},{5,7},{6,4},{7,5},{8,10},{9,11},{10,... | collective-permute-start | bytes 6152 | tf_op jit(solution)/shard_map/ppermute | solution.py:12
  55.6 3.7 %collective-permute-start.4 = (f32[32,16]{0,1:T(8,128)S(1)}, f32[32,16]{0,1:T(8,128)S(1)}, u32[]{:S(2)}, u32[]{:S(2)}) collective-permute-start(f32[32,16]{0,1:T(8,128)S(1)} %slice_select_fusion.10), channel_id=1, source_target_pairs={{0,2},{1,3},{2,0},{3,1},{4,6},{5,7},{6,4},{7,5},{8,10},{9,11},{10,... | collective-permute-start | bytes 6152 | tf_op jit(solution)/shard_map/ppermute | solution.py:12
  73.0 1.5 copy-start.3
  76.2 7.1 %collective-permute-start.5 = (f32[32,2560]{1,0:T(8,128)S(1)}, f32[32,2560]{1,0:T(8,128)S(1)}, u32[]{:S(2)}, u32[]{:S(2)}) collective-permute-start(f32[32,2560]{1,0:T(8,128)S(1)} %copy.44), channel_id=1, source_target_pairs={{0,2},{1,3},{2,0},{3,1},{4,6},{5,7},{6,4},{7,5},{8,10},{9,11},{10,... | collective-permute-start | bytes 983048 | tf_op jit(solution)/shard_map/ppermute | solution.py:12
  77.8 12.8 %collective-permute-start.11 = (f32[16,16]{0,1:T(8,128)S(1)}, f32[16,16]{0,1:T(8,128)S(1)}, u32[]{:S(2)}, u32[]{:S(2)}) collective-permute-start(f32[16,16]{0,1:T(8,128)S(1)} %slice_select_fusion.4), channel_id=1, source_target_pairs={{0,1},{1,0},{2,3},{3,2},{4,5},{5,4},{6,7},{7,6},{8,9},{9,8},{10,11... | collective-permute-start | bytes 3080 | tf_op jit(solution)/shard_map/ppermute | solution.py:12
  77.9 12.7 %collective-permute-start.6 = (f32[16,16]{0,1:T(8,128)S(1)}, f32[16,16]{0,1:T(8,128)S(1)}, u32[]{:S(2)}, u32[]{:S(2)}) collective-permute-start(f32[16,16]{0,1:T(8,128)S(1)} %slice_select_fusion.8), channel_id=1, source_target_pairs={{0,1},{1,0},{2,3},{3,2},{4,5},{5,4},{6,7},{7,6},{8,9},{9,8},{10,11... | collective-permute-start | bytes 3080 | tf_op jit(solution)/shard_map/ppermute | solution.py:12
  87.3 1.5 copy-start.2
  90.5 1.4 collective-permute-start.7
  97.1 1.7 copy-start.6
  99.0 5.4 %collective-permute-start.12 = (bf16[16,2688]{1,0:T(8,128)(2,1)S(1)}, bf16[16,2688]{1,0:T(8,128)(2,1)S(1)}, u32[]{:S(2)}, u32[]{:S(2)}) collective-permute-start(bf16[16,2688]{1,0:T(8,128)(2,1)S(1)} %concatenate.22), channel_id=1, source_target_pairs={{0,16},{1,9},{2,18},{3,11},{4,20},{5,13},{6,22},{7,15},{8,24},{9,1... | collective-permute-start | bytes 258056 | tf_op jit(solution)/shard_map/ppermute | solution.py:27
  104.4 6.4 %collective-permute-start.13 = (bf16[32,2688]{1,0:T(8,128)(2,1)S(1)}, bf16[32,2688]{1,0:T(8,128)(2,1)S(1)}, u32[]{:S(2)}, u32[]{:S(2)}) collective-permute-start(bf16[32,2688]{1,0:T(8,128)(2,1)S(1)} %pad_maximum_fusion.2), channel_id=1, source_target_pairs={{0,8},{1,17},{2,10},{3,19},{4,12},{5,21},{6,14},{7,23},{8,0},{9,25... | collective-permute-start | bytes 516104 | tf_op jit(solution)/shard_map/ppermute | solution.py:27
  110.8 7.3 %collective-permute-start.14 = (bf16[64,2688]{1,0:T(8,128)(2,1)S(1)}, bf16[64,2688]{1,0:T(8,128)(2,1)S(1)}, u32[]{:S(2)}, u32[]{:S(2)}) collective-permute-start(bf16[64,2688]{1,0:T(8,128)(2,1)S(1)} %pad_maximum_fusion.1), channel_id=1, source_target_pairs={{0,4},{1,3},{2,6},{3,1},{4,0},{5,7},{6,2},{7,5},{8,12},{9,11},{10,... | collective-permute-start | bytes 1032200 | tf_op jit(solution)/shard_map/ppermute | solution.py:27
  118.2 11.0 %collective-permute-start.15 = (bf16[128,2688]{1,0:T(8,128)(2,1)S(1)}, bf16[128,2688]{1,0:T(8,128)(2,1)S(1)}, u32[]{:S(2)}, u32[]{:S(2)}) collective-permute-start(bf16[128,2688]{1,0:T(8,128)(2,1)S(1)} %pad_maximum_fusion), channel_id=1, source_target_pairs={{0,2},{1,5},{2,0},{3,7},{4,6},{5,1},{6,4},{7,3},{8,10},{9,13},{10,... | collective-permute-start | bytes 2064392 | tf_op jit(solution)/shard_map/ppermute | solution.py:27
  129.4 3.2 %collective-permute-start.16 = (bf16[256,2688]{1,0:T(8,128)(2,1)S(1)}, bf16[256,2688]{1,0:T(8,128)(2,1)S(1)}, u32[]{:S(2)}, u32[]{:S(2)}) collective-permute-start(bf16[256,2688]{1,0:T(8,128)(2,1)S(1)} %get-tuple-element.24), channel_id=1, source_target_pairs={{0,1},{1,0},{2,3},{3,2},{4,5},{5,4},{6,7},{7,6},{8,9},{9,8},{10,11... | collective-permute-start | bytes 4128776 | tf_op jit(solution)/shard_map/ppermute | solution.py:12
  132.6 1.7 copy-start.9
  134.3 2.6 %copy-start.5 = (bf16[512,2688]{1,0:T(8,128)(2,1)}, bf16[512,2688]{1,0:T(8,128)(2,1)S(1)}, u32[]{:S(2)}) copy-start(bf16[512,2688]{1,0:T(8,128)(2,1)S(1)} %constant_dynamic-update-slice_fusion.5) | copy-start | bytes 8257540
  147.2 3.1 %collective-permute-start.17 = (bf16[256,2560]{1,0:T(8,128)(2,1)S(1)}, bf16[256,2560]{1,0:T(8,128)(2,1)S(1)}, u32[]{:S(2)}, u32[]{:S(2)}) collective-permute-start(bf16[256,2560]{1,0:T(8,128)(2,1)S(1)} %slice.325), channel_id=1, source_target_pairs={{0,1},{1,0},{2,3},{3,2},{4,5},{5,4},{6,7},{7,6},{8,9},{9,8},{10,11... | collective-permute-start | bytes 3932168 | tf_op jit(solution)/shard_map/ppermute | solution.py:12
  152.5 10.7 %collective-permute-start.18 = (bf16[128,2560]{1,0:T(8,128)(2,1)S(1)}, bf16[128,2560]{1,0:T(8,128)(2,1)S(1)}, u32[]{:S(2)}, u32[]{:S(2)}) collective-permute-start(bf16[128,2560]{1,0:T(8,128)(2,1)S(1)} %slice.326), channel_id=1, source_target_pairs={{0,2},{1,5},{2,0},{3,7},{4,6},{5,1},{6,4},{7,3},{8,10},{9,13},{10,... | collective-permute-start | bytes 1966088 | tf_op jit(solution)/shard_map/ppermute | solution.py:27
  163.3 7.1 %collective-permute-start.19 = (bf16[64,2560]{1,0:T(8,128)(2,1)S(1)}, bf16[64,2560]{1,0:T(8,128)(2,1)S(1)}, u32[]{:S(2)}, u32[]{:S(2)}) collective-permute-start(bf16[64,2560]{1,0:T(8,128)(2,1)S(1)} %slice.327), channel_id=1, source_target_pairs={{0,4},{1,3},{2,6},{3,1},{4,0},{5,7},{6,2},{7,5},{8,12},{9,11},{10,... | collective-permute-start | bytes 983048 | tf_op jit(solution)/shard_map/ppermute | solution.py:27
  170.6 5.7 %collective-permute-start.20 = (bf16[32,2560]{1,0:T(8,128)(2,1)S(1)}, bf16[32,2560]{1,0:T(8,128)(2,1)S(1)}, u32[]{:S(2)}, u32[]{:S(2)}) collective-permute-start(bf16[32,2560]{1,0:T(8,128)(2,1)S(1)} %slice.328), channel_id=1, source_target_pairs={{0,8},{1,17},{2,10},{3,19},{4,12},{5,21},{6,14},{7,23},{8,0},{9,25... | collective-permute-start | bytes 491528 | tf_op jit(solution)/shard_map/ppermute | solution.py:27
  176.3 5.7 %collective-permute-start.21 = (bf16[16,2560]{1,0:T(8,128)(2,1)S(1)}, bf16[16,2560]{1,0:T(8,128)(2,1)S(1)}, u32[]{:S(2)}, u32[]{:S(2)}) collective-permute-start(bf16[16,2560]{1,0:T(8,128)(2,1)S(1)} %slice.329), channel_id=1, source_target_pairs={{0,16},{1,9},{2,18},{3,11},{4,20},{5,13},{6,22},{7,15},{8,24},{9,1... | collective-permute-start | bytes 245768 | tf_op jit(solution)/shard_map/ppermute | solution.py:27

commit v2 on v1

v2 whole, which is shorter than its diff:
```python
import functools

import jax
import jax.numpy as jnp
from jax import lax
from jax.experimental import pallas as pl
from jax.experimental.pallas import tpu as pltpu
from jax.sharding import PartitionSpec as P

HEADS = 16
LANES = 128


def partner(value, axis, stride):
    mask = 2**stride
    pairs = [(source, source ^ mask) for source in range(lax.axis_size(axis))]
    return lax.ppermute(value, axis, pairs)


def stage_orders(devices):
    bits = list(reversed(range(1, devices.bit_length() - 1)))
    other = bits[:-2] + bits[-2:][::-1]
    other = other[:2][::-1] + other[2:] if len(other) > 3 else other
    return (bits, other)


def merge_orders(group_size):
    bits = list(range(1, group_size.bit_length() - 1))
    return (bits, bits[1:] + bits[:1])


def exchange(value, orders, stage):
    pairs = [
        (source, source ^ (1 << orders[source % 2][stage]))
        for source in range(lax.axis_size("wide"))
    ]
    return lax.ppermute(value, "wide", pairs)


def lane_iota(shape):
    return lax.broadcasted_iota(jnp.int32, shape, 1)


def expand_tile(columns, tile, value_size):
    first = tile * LANES // value_size
    last = (tile * LANES + LANES - 1) // value_size
    rows = columns[0].shape[0]
    out = jnp.broadcast_to(columns[first], (rows, LANES))
    for head in range(first + 1, last + 1):
        edge = head * value_size - tile * LANES
        out = jnp.where(lane_iota((rows, LANES)) < edge, out, columns[head])
    return out


def pack_stats(peak, total, head_count):
    lane = lane_iota(peak.shape)
    high = total.astype(jnp.bfloat16).astype(jnp.float32)
    low = total - high
    packed = jnp.where(lane < head_count, peak, 0.0)
    shifted = pltpu.roll(jnp.where(lane < head_count, high, 0.0), head_count, 1)
    shifted_low = pltpu.roll(jnp.where(lane < head_count, low, 0.0), 2 * head_count, 1)
    return packed + shifted + shifted_low


def total_of(stats, head_count):
    return pltpu.roll(stats, LANES - head_count, 1) + pltpu.roll(
        stats, LANES - 2 * head_count, 1
    )


def attend_kernel(
    head_count,
    row_count,
    blocks_ref,
    queries_ref,
    keys_a_ref,
    keys_b_ref,
    values_a_ref,
    values_b_ref,
    sent_ref,
    kept_ref,
    query_scratch,
):
    block_count = blocks_ref.shape[0]
    rows = block_count * row_count
    half = rows // 2
    vision_width = queries_ref.shape[1]
    model_width = values_a_ref.shape[1]
    key_size = vision_width // head_count
    value_size = model_width // head_count
    scale = key_size ** (-0.5)
    for slot in range(block_count):
        start = pl.multiple_of(blocks_ref[slot] * row_count, row_count)
        query_scratch[slot * row_count : (slot + 1) * row_count, :] = queries_ref[
            pl.ds(start, row_count), :
        ]
    peaks = jnp.zeros((rows, LANES), jnp.float32)
    totals = jnp.zeros((rows, LANES), jnp.float32)
    lane = lane_iota((rows, LANES))
    contract_last = (((1,), (1,)), ((), ()))
    contract_rows = (((1,), (0,)), ((), ()))
    waiting = None

    def put(tile, value):
        columns = slice(tile * LANES, (tile + 1) * LANES)
        kept_ref[:, columns] = value[:half]
        sent_ref[:, columns] = value[half:].astype(jnp.bfloat16)

    for head in range(head_count):
        low = head * key_size // LANES * LANES
        high = -(-(head + 1) * key_size // LANES) * LANES
        window = lane_iota((rows, high - low)) + low
        inside = (window >= head * key_size) & (window < (head + 1) * key_size)
        query = jnp.where(inside, query_scratch[:, low:high], jnp.zeros((), jnp.bfloat16))
        score_a = scale * lax.dot_general(
            query, keys_a_ref[:, low:high], contract_last, preferred_element_type=jnp.float32
        )
        score_b = scale * lax.dot_general(
            query, keys_b_ref[:, low:high], contract_last, preferred_element_type=jnp.float32
        )
        peak = jnp.maximum(
            jnp.max(score_a, axis=1, keepdims=True), jnp.max(score_b, axis=1, keepdims=True)
        )
        peak = peak.astype(jnp.bfloat16).astype(jnp.float32)
        raised_a = jnp.exp(score_a - peak)
        raised_b = jnp.exp(score_b - peak)
        total = jnp.sum(raised_a, axis=1, keepdims=True) + jnp.sum(
            raised_b, axis=1, keepdims=True
        )
        peaks = jnp.where(lane == head, peak, peaks)
        totals = jnp.where(lane == head, total, totals)
        low = head * value_size // LANES
        high = -(-(head + 1) * value_size // LANES)
        summed = lax.dot_general(
            raised_a.astype(jnp.bfloat16),
            values_a_ref[:, low * LANES : high * LANES],
            contract_rows,
            preferred_element_type=jnp.float32,
        ) + lax.dot_general(
            raised_b.astype(jnp.bfloat16),
            values_b_ref[:, low * LANES : high * LANES],
            contract_rows,
            preferred_element_type=jnp.float32,
        )
        for tile in range(low, high):
            value = summed[:, (tile - low) * LANES : (tile - low + 1) * LANES]
            edge = head * value_size - tile * LANES
            if edge > 0:
                value = jnp.where(lane < edge, waiting, value)
            if (tile + 1) * LANES > (head + 1) * value_size:
                waiting = value
            else:
                put(tile, value)
    put(model_width // LANES, pack_stats(peaks, totals, head_count))


def merged_parts(kept_ref, came_ref, head_count, model_width):
    stats_a = kept_ref[:, model_width:]
    stats_b = came_ref[:, model_width:].astype(jnp.float32)
    peak = jnp.maximum(stats_a, stats_b)
    factor_a = jnp.exp(stats_a - peak)
    factor_b = jnp.exp(stats_b - peak)
    total = total_of(stats_a, head_count) * factor_a + total_of(stats_b, head_count) * factor_b
    return peak, total, factor_a, factor_b


def head_columns(array, head_count):
    return [array[:, head : head + 1] for head in range(head_count)]


def merge_kernel(head_count, kept_ref, came_ref, sent_ref, next_ref):
    model_width = kept_ref.shape[1] - LANES
    half = kept_ref.shape[0] // 2
    peak, total, factor_a, factor_b = merged_parts(kept_ref, came_ref, head_count, model_width)
    columns_a = head_columns(factor_a, head_count)
    columns_b = head_columns(factor_b, head_count)
    for tile in range(model_width // LANES + 1):
        columns = slice(tile * LANES, (tile + 1) * LANES)
        if tile * LANES == model_width:
            value = pack_stats(peak, total, head_count)
        else:
            value = kept_ref[:, columns] * expand_tile(
                columns_a, tile, model_width // head_count
            ) + came_ref[:, columns].astype(jnp.float32) * expand_tile(
                columns_b, tile, model_width // head_count
            )
        next_ref[:, columns] = value[:half]
        sent_ref[:, columns] = value[half:].astype(jnp.bfloat16)


def finish_kernel(head_count, kept_ref, came_ref, gain_ref, table_ref, block_ref, projected_ref):
    model_width = kept_ref.shape[1] - LANES
    _, total, factor_a, factor_b = merged_parts(kept_ref, came_ref, head_count, model_width)
    columns_a = head_columns(factor_a / total, head_count)
    columns_b = head_columns(factor_b / total, head_count)
    square = jnp.zeros((kept_ref.shape[0], LANES), jnp.float32)
    for tile in range(model_width // LANES):
        columns = slice(tile * LANES, (tile + 1) * LANES)
        value = kept_ref[:, columns] * expand_tile(
            columns_a, tile, model_width // head_count
        ) + came_ref[:, columns].astype(jnp.float32) * expand_tile(
            columns_b, tile, model_width // head_count
        )
        rounded = value.astype(jnp.bfloat16)
        projected_ref[:, columns] = rounded
        residual = rounded.astype(jnp.float32)
        square = square + residual * residual
    mean = jnp.sum(square, axis=1, keepdims=True) / model_width
    inverse = lax.rsqrt(mean + 1e-06)
    normed = projected_ref[...].astype(jnp.float32) * inverse * gain_ref[...]
    block_ref[:, :model_width] = normed.astype(jnp.bfloat16)
    block_ref[:, model_width:] = table_ref[...]


def attention_rows(queries, patch_keys, patch_values, norm_gain, table, row_count):
    model_width = patch_values.shape[1]
    packed_width = model_width + LANES
    group_size = queries.shape[0] // row_count
    orders = merge_orders(group_size)
    stages = len(orders[0])
    device_index = lax.axis_index("wide")
    masks = [
        [
            sum(
                (1 << order[stage])
                for stage in range(stages)
                if slot >> (stages - 1 - stage) & 1
            )
            for slot in range(1 << stages)
        ]
        for order in orders
    ]
    masks = jnp.array(masks, jnp.int32)
    blocks = (device_index % group_size) ^ jnp.where(device_index % 2 == 1, masks[1], masks[0])
    rows = row_count << stages
    other_keys = partner(patch_keys, "wide", 0)
    other_values = partner(patch_values, "wide", 0)
    whole = pl.BlockSpec(memory_space=pltpu.VMEM)

    def pair_shapes(rows):
        return (
            jax.ShapeDtypeStruct((rows, packed_width), jnp.bfloat16),
            jax.ShapeDtypeStruct((rows, packed_width), jnp.float32),
        )

    sent, kept = pl.pallas_call(
        functools.partial(attend_kernel, HEADS, row_count),
        name="attend",
        out_shape=pair_shapes(rows // 2),
        in_specs=[pl.BlockSpec(memory_space=pltpu.SMEM)] + [whole] * 5,
        out_specs=(whole, whole),
        scratch_shapes=[pltpu.VMEM((rows, queries.shape[1]), jnp.bfloat16)],
    )(blocks, queries, patch_keys, other_keys, patch_values, other_values)
    for stage in range(stages - 1):
        came = exchange(sent, orders, stage)
        sent, kept = pl.pallas_call(
            functools.partial(merge_kernel, HEADS),
            name="merge",
            out_shape=pair_shapes(kept.shape[0] // 2),
            in_specs=[whole] * 2,
            out_specs=(whole, whole),
        )(kept, came)
    came = exchange(sent, orders, stages - 1)
    return pl.pallas_call(
        functools.partial(finish_kernel, HEADS),
        name="finish",
        out_shape=(
            jax.ShapeDtypeStruct((row_count, packed_width), jnp.bfloat16),
            jax.ShapeDtypeStruct((row_count, model_width), jnp.bfloat16),
        ),
        in_specs=[whole] * 4,
        out_specs=(whole, whole),
    )(kept, came, norm_gain.reshape(1, model_width), table)


def on_device(
    queries, patch_keys, patch_values, norm_gain, route_experts, route_weights, w_gate, w_up, w_down
):
    row_count = route_experts.shape[0]
    model_width = patch_values.shape[1]
    devices = lax.axis_size("wide")
    device_index = lax.axis_index("wide")
    experts = devices // 2
    score_table = jnp.sum(
        jnp.where(
            route_experts[:, :, None] == jnp.arange(LANES, dtype=jnp.int32)[None, None, :],
            route_weights[:, :, None],
            0,
        ),
        axis=1,
    ).astype(jnp.bfloat16)
    block, projected = attention_rows(
        queries, patch_keys, patch_values, norm_gain, score_table, row_count
    )
    orders = stage_orders(devices)
    for stage in range(len(orders[0])):
        block = jnp.concatenate([block, exchange(block, orders, stage)], axis=0)
    block = jnp.concatenate([block, partner(block, "wide", 0)], axis=0)
    rows_in = block[:, :model_width]
    score_rows = block[:, model_width : model_width + experts].astype(jnp.float32)
    own_expert = jnp.arange(experts, dtype=jnp.int32)[None, :] == device_index // 2
    share = jnp.sum(jnp.where(own_expert, score_rows, 0.0), axis=1, keepdims=True) / jnp.sum(
        score_rows, axis=1, keepdims=True
    )
    gate_part = lax.dot_general(
        rows_in, w_gate, (((1,), (1,)), ((), ())), preferred_element_type=jnp.float32
    )
    up_part = lax.dot_general(
        rows_in, w_up, (((1,), (1,)), ((), ())), preferred_element_type=jnp.float32
    )
    hidden = (jax.nn.silu(gate_part) * up_part * share).astype(jnp.bfloat16)
    partial_value = lax.dot_general(
        hidden, w_down, (((1,), (0,)), ((), ())), preferred_element_type=jnp.float32
    )
    half_rows = partial_value.shape[0] // 2
    total = partial_value[:half_rows] + partner(
        partial_value[half_rows:].astype(jnp.bfloat16), "wide", 0
    ).astype(jnp.float32)
    for stage in reversed(range(len(orders[0]))):
        half_rows = total.shape[0] // 2
        total = total[:half_rows] + exchange(
            total[half_rows:].astype(jnp.bfloat16), orders, stage
        ).astype(jnp.float32)
    return (projected.astype(jnp.float32) + total).astype(jnp.bfloat16)


def solution(mesh):
    return jax.shard_map(
        on_device,
        mesh=mesh,
        in_specs=(
            P("groups", None),
            P(("groups", "wide"), None),
            P(("groups", "wide"), None),
            P(),
            P(("groups", "wide"), None),
            P(("groups", "wide"), None),
            P("wide", None),
            P("wide", None),
            P("wide", None),
        ),
        out_specs=P(("groups", "wide"), None),
        check_vma=False,
    )
```

time: 183 us -> 134 us (0.73)
  waiting for transfers between devices: 99.9 us -> 56.9 us
  other arithmetic: 21.7 us -> 8.76 us
  Pallas kernels: 0 us -> 10.6 us
  local copies, waits for them, and re-layouts: 22.5 us -> 14.2 us
  starting transfers between devices: 25.2 us -> 30.2 us
    ppermute x14 -> x4, waiting for transfers between devices: 54 us -> 7.52 us  [partner(): return lax.ppermute(value, axis, pairs)]
    ppermute x8 -> x11, starting transfers between devices: 13.2 us -> 29.4 us  [exchange(): return lax.ppermute(value, 'wide', pairs)]
    ppermute x14 -> x4, starting transfers between devices: 12 us -> 0.85 us  [partner(): return lax.ppermute(value, axis, pairs)]
    pallas_call x0 -> x4, Pallas kernels: none -> 10.6 us  [the longest x2 4.4 us: attention_rows(): pl.pallas_call(functools.partial(merge_kernel, HEADS), name='merge', out_...]
    add x7 -> x0, other arithmetic: 7.87 us -> none  [the longest x3 7.61 us: merge_partials(): summed + sum_second.reshape(row_count, head_count, -1) * factor_second[:,...]
    select_n x12 -> x0, other arithmetic: 6.24 us -> none  [the longest x4 5.79 us: on_device(): sent_sum = jnp.where(upper_half, summed[:half_rows], summed[half_rows:])]
    ppermute x3 -> x0, local copies, waits for them, and re-layouts: 5.46 us -> none  [partner(): return lax.ppermute(value, axis, pairs)]
    select_n x3 -> x0, local copies, waits for them, and re-layouts: 5.09 us -> none  [on_device(): sent_sum = jnp.where(upper_half, summed[:half_rows], summed[half_rows:])]
  transfers between devices with their start and end apart: 22 -> 15, of which waited for: 19 -> 14; matrix products, arithmetic and copies ran while one was open for 5% -> 5% of each run, Pallas kernels for 0% -> 0%
where the time goes in v2:
time: 134 us; the launch traced here: 133 us
  waiting for transfers between devices  56.9 us (42%)
  starting transfers between devices  30.2 us (23%)
  local copies, waits for them, and re-layouts  14.2 us (11%)
  matrix products  12.5 us (9%)
  Pallas kernels  10.6 us (8%)
  other arithmetic  8.76 us (7%)
    ppermute x11, waiting for transfers between devices, exchange(): return lax.ppermute(value, 'wide', pairs)  49.4 us
    ppermute x11, starting transfers between devices, exchange(): return lax.ppermute(value, 'wide', pairs)  29.4 us
    dot_general x1, matrix products, on_device(): lax.dot_general(hidden, w_down, (((1,), (0,)), ((), ())), preferred_eleme...  8.2 us
    unnamed x26, local copies, waits for them, and re-layouts  8.11 us
    ppermute x4, waiting for transfers between devices, partner(): return lax.ppermute(value, axis, pairs)  7.52 us
    pallas_call x2, Pallas kernels, attention_rows(): pl.pallas_call(functools.partial(merge_kernel, HEADS), name='merge', out_...  4.4 us
    dot_general x1, matrix products, on_device(): lax.dot_general(rows_in, w_up, (((1,), (1,)), ((), ())), preferred_elemen...  4.33 us
    pallas_call x1, Pallas kernels, attention_rows(): pl.pallas_call(functools.partial(attend_kernel, HEADS, row_count), name='...  4.24 us
  transfers between devices with their start and end apart: 15, of which 14 were waited for; matrix products, arithmetic and copies ran while one was open for 5% of the time, Pallas kernels for 0%

profile of v2, /device:TPU:0, one launch (start us, length us, event | category | flops | bytes accessed | tf_op | source)
XLA Modules:
  0.0 133.3 jit_solution(12283558994911822810)
XLA Ops:
  4.0 4.2 %attend.1 = (bf16[64,2688]{1,0:T(8,128)(2,1)}, f32[64,2688]{1,0:T(8,128)}) custom-call(s32[8]{0:T(128)} %fusion.15.blocks_ref, bf16[256,1152]{1,0:T(8,128)(2,1)} %queries_ref.1, bf16[128,1152]{1,0:T(8,128)(2,1)} %keys_a_ref.1, bf16[128,1152]{1,0:T(8,128)(2,1)} %collective-permute-done.keys_b_ref, bf16[128,2560]{1,0:T(8,128)(2,1)} %values_a_ref.1, ...), custom_call_target="tpu_custom_call" | custom-call | tf_op jit(solution)/shard_map/attend/pallas_call | solution.py:246
  8.2 2.9 %collective-permute-start.2 = (bf16[64,2688]{1,0:T(8,128)(2,1)}, bf16[64,2688]{1,0:T(8,128)(2,1)S(1)}, u32[]{:S(2)}, u32[]{:S(2)}) collective-permute-start(bf16[64,2688]{1,0:T(8,128)(2,1)} %get-tuple-element.14), channel_id=1, source_target_pairs={{0,2},{1,5},{2,0},{3,7},{4,6},{5,1},{6,4},{7,3},{8,10},{9,13},{10,... | collective-permute-start | bytes 1032200 | tf_op jit(solution)/shard_map/ppermute | solution.py:37
  11.1 5.4 %collective-permute-done.2.came_ref = bf16[64,2688]{1,0:T(8,128)(2,1)S(1)} collective-permute-done((bf16[64,2688]{1,0:T(8,128)(2,1)}, bf16[64,2688]{1,0:T(8,128)(2,1)S(1)}, u32[]{:S(2)}, u32[]{:S(2)}) %collective-permute-start.2) | collective-permute-done | bytes 344096 | tf_op jit(solution)/shard_map/ppermute | solution.py:37
  17.2 2.4 %merge.2 = (bf16[32,2688]{1,0:T(8,128)(2,1)}, f32[32,2688]{1,0:T(8,128)}) custom-call(f32[64,2688]{1,0:T(8,128)} %get-tuple-element.13.kept_ref, bf16[64,2688]{1,0:T(8,128)(2,1)} %copy-done.2), custom_call_target="tpu_custom_call" | custom-call | tf_op jit(solution)/shard_map/merge/pallas_call | solution.py:256
  19.6 2.0 %collective-permute-start.3 = (bf16[32,2688]{1,0:T(8,128)(2,1)}, bf16[32,2688]{1,0:T(8,128)(2,1)S(1)}, u32[]{:S(2)}, u32[]{:S(2)}) collective-permute-start(bf16[32,2688]{1,0:T(8,128)(2,1)} %get-tuple-element.16), channel_id=1, source_target_pairs={{0,4},{1,9},{2,6},{3,11},{4,0},{5,13},{6,2},{7,15},{8,12},{9,1},{1... | collective-permute-start | bytes 516104 | tf_op jit(solution)/shard_map/ppermute | solution.py:37
  22.3 3.0 %collective-permute-done.3.came_ref = bf16[32,2688]{1,0:T(8,128)(2,1)S(1)} collective-permute-done((bf16[32,2688]{1,0:T(8,128)(2,1)}, bf16[32,2688]{1,0:T(8,128)(2,1)S(1)}, u32[]{:S(2)}, u32[]{:S(2)}) %collective-permute-start.3) | collective-permute-done | bytes 172064 | tf_op jit(solution)/shard_map/ppermute | solution.py:37
  25.9 2.0 %merge.3 = (bf16[16,2688]{1,0:T(8,128)(2,1)}, f32[16,2688]{1,0:T(8,128)}) custom-call(f32[32,2688]{1,0:T(8,128)} %get-tuple-element.15.kept_ref, bf16[32,2688]{1,0:T(8,128)(2,1)} %copy-done.3), custom_call_target="tpu_custom_call" | custom-call | tf_op jit(solution)/shard_map/merge/pallas_call | solution.py:256
  27.9 2.1 %collective-permute-start.4 = (bf16[16,2688]{1,0:T(8,128)(2,1)}, bf16[16,2688]{1,0:T(8,128)(2,1)S(1)}, u32[]{:S(2)}, u32[]{:S(2)}) collective-permute-start(bf16[16,2688]{1,0:T(8,128)(2,1)} %get-tuple-element.18), channel_id=1, source_target_pairs={{0,8},{1,3},{2,10},{3,1},{4,12},{5,7},{6,14},{7,5},{8,0},{9,11},{1... | collective-permute-start | bytes 258056 | tf_op jit(solution)/shard_map/ppermute | solution.py:37
  30.7 2.0 %collective-permute-done.4.came_ref = bf16[16,2688]{1,0:T(8,128)(2,1)S(1)} collective-permute-done((bf16[16,2688]{1,0:T(8,128)(2,1)}, bf16[16,2688]{1,0:T(8,128)(2,1)S(1)}, u32[]{:S(2)}, u32[]{:S(2)}) %collective-permute-start.4) | collective-permute-done | bytes 86048 | tf_op jit(solution)/shard_map/ppermute | solution.py:37
  33.3 1.9 %finish.1 = (bf16[16,2688]{1,0:T(8,128)(2,1)}, bf16[16,2560]{1,0:T(8,128)(2,1)}) custom-call(f32[16,2688]{1,0:T(8,128)} %get-tuple-element.17.kept_ref, bf16[16,2688]{1,0:T(8,128)(2,1)} %copy-done.4, f32[1,2560]{1,0:T(1,128)} %reshape.20.gain_ref, bf16[16,128]{1,0:T(8,128)(2,1)} %convert_element_type.35.table_ref), custom_call_target="tpu_custom_call" | custom-call | tf_op jit(solution)/shard_map/finish/pallas_call | solution.py:264
  35.3 3.0 %collective-permute-start.5 = (bf16[16,2688]{1,0:T(8,128)(2,1)}, bf16[16,2688]{1,0:T(8,128)(2,1)S(1)}, u32[]{:S(2)}, u32[]{:S(2)}) collective-permute-start(bf16[16,2688]{1,0:T(8,128)(2,1)} %get-tuple-element.20), channel_id=1, source_target_pairs={{0,16},{1,9},{2,18},{3,11},{4,20},{5,13},{6,22},{7,15},{8,24},{9,1... | collective-permute-start | bytes 258056 | tf_op jit(solution)/shard_map/ppermute | solution.py:37
  38.3 2.7 %collective-permute-done.5 = bf16[16,2688]{1,0:T(8,128)(2,1)S(1)} collective-permute-done((bf16[16,2688]{1,0:T(8,128)(2,1)}, bf16[16,2688]{1,0:T(8,128)(2,1)S(1)}, u32[]{:S(2)}, u32[]{:S(2)}) %collective-permute-start.5) | collective-permute-done | bytes 86048 | tf_op jit(solution)/shard_map/ppermute | solution.py:37
  41.9 4.8 %collective-permute-start.6 = (bf16[32,2688]{1,0:T(8,128)(2,1)S(1)}, bf16[32,2688]{1,0:T(8,128)(2,1)S(1)}, u32[]{:S(2)}, u32[]{:S(2)}) collective-permute-start(bf16[32,2688]{1,0:T(8,128)(2,1)S(1)} %pad_maximum_fusion.2), channel_id=1, source_target_pairs={{0,8},{1,17},{2,10},{3,19},{4,12},{5,21},{6,14},{7,23},{8,0},{9,25... | collective-permute-start | bytes 516104 | tf_op jit(solution)/shard_map/ppermute | solution.py:37
  46.7 3.4 %collective-permute-done.6 = bf16[32,2688]{1,0:T(8,128)(2,1)S(1)} collective-permute-done((bf16[32,2688]{1,0:T(8,128)(2,1)S(1)}, bf16[32,2688]{1,0:T(8,128)(2,1)S(1)}, u32[]{:S(2)}, u32[]{:S(2)}) %collective-permute-start.6) | collective-permute-done | bytes 172064 | tf_op jit(solution)/shard_map/ppermute | solution.py:37
  51.0 2.3 %collective-permute-start.7 = (bf16[64,2688]{1,0:T(8,128)(2,1)S(1)}, bf16[64,2688]{1,0:T(8,128)(2,1)S(1)}, u32[]{:S(2)}, u32[]{:S(2)}) collective-permute-start(bf16[64,2688]{1,0:T(8,128)(2,1)S(1)} %pad_maximum_fusion.1), channel_id=1, source_target_pairs={{0,4},{1,3},{2,6},{3,1},{4,0},{5,7},{6,2},{7,5},{8,12},{9,11},{10,... | collective-permute-start | bytes 1032200 | tf_op jit(solution)/shard_map/ppermute | solution.py:37
  55.4 5.3 %collective-permute-done.7 = bf16[64,2688]{1,0:T(8,128)(2,1)S(1)} collective-permute-done((bf16[64,2688]{1,0:T(8,128)(2,1)S(1)}, bf16[64,2688]{1,0:T(8,128)(2,1)S(1)}, u32[]{:S(2)}, u32[]{:S(2)}) %collective-permute-start.7) | collective-permute-done | bytes 344096 | tf_op jit(solution)/shard_map/ppermute | solution.py:37
  61.7 2.4 %collective-permute-start.8 = (bf16[128,2688]{1,0:T(8,128)(2,1)S(1)}, bf16[128,2688]{1,0:T(8,128)(2,1)S(1)}, u32[]{:S(2)}, u32[]{:S(2)}) collective-permute-start(bf16[128,2688]{1,0:T(8,128)(2,1)S(1)} %pad_maximum_fusion), channel_id=1, source_target_pairs={{0,2},{1,5},{2,0},{3,7},{4,6},{5,1},{6,4},{7,3},{8,10},{9,13},{10,... | collective-permute-start | bytes 2064392 | tf_op jit(solution)/shard_map/ppermute | solution.py:37
  65.5 7.5 %collective-permute-done.8 = bf16[128,2688]{1,0:T(8,128)(2,1)S(1)} collective-permute-done((bf16[128,2688]{1,0:T(8,128)(2,1)S(1)}, bf16[128,2688]{1,0:T(8,128)(2,1)S(1)}, u32[]{:S(2)}, u32[]{:S(2)}) %collective-permute-start.8) | collective-permute-done | bytes 688160 | tf_op jit(solution)/shard_map/ppermute | solution.py:37
  75.5 3.5 %collective-permute-done.9 = bf16[256,2688]{1,0:T(8,128)(2,1)} collective-permute-done((bf16[256,2688]{1,0:T(8,128)(2,1)}, bf16[256,2688]{1,0:T(8,128)(2,1)}, u32[]{:S(2)}, u32[]{:S(2)}) %collective-permute-start.9) | collective-permute-done | bytes 1376288 | tf_op jit(solution)/shard_map/ppermute | solution.py:17
  79.0 2.5 %constant_dynamic-update-slice_fusion.5 = bf16[512,2688]{1,0:T(8,128)(2,1)} fusion(bf16[512,2688]{1,0:T(8,128)(2,1)} %copy-done.6, bf16[256,2688]{1,0:T(8,128)(2,1)} %collective-permute-done.9), kind=kLoop, calls=%fused_computation.33 | loop fusion | bytes 2752512 | tf_op jit(solution)/shard_map/concatenate | solution.py:298
  81.5 4.3 %fusion = f32[512,512]{1,0:T(8,128)} fusion(bf16[512,2560]{1,0:T(8,128)(2,1)S(1)} %copy-done.10, bf16[512,2688]{1,0:T(8,128)(2,1)} %constant_dynamic-update-slice_fusion.5), kind=kOutput, calls=%fused_computation.2 | convolution fusion | flops 1342177280 | bytes 6291456 | tf_op jit(solution)/shard_map/dot_general | solution.py:308
  86.9 8.2 %fusion.4 = f32[512,2560]{1,0:T(8,128)} fusion(bf16[512,2560]{1,0:T(8,128)(2,1)S(1)} %copy-done, f32[512,512]{1,0:T(8,128)} %fusion, bf16[512,2560]{1,0:T(8,128)(2,1)} %param.16, bf16[512,2688]{1,0:T(8,128)(2,1)} %constant_dynamic-update-slice_fusion.5, f32[512]{0:T(512)S(1)} %div.24), kind=kOutput, calls=%fused_computation.12 | convolution fusion | flops 2686189568 | bytes 14157824 | tf_op jit(solution)/shard_map/dot_general | solution.py:312
  97.2 2.9 %collective-permute-done.10 = bf16[256,2560]{1,0:T(8,128)(2,1)S(1)} collective-permute-done((bf16[256,2560]{1,0:T(8,128)(2,1)S(1)}, bf16[256,2560]{1,0:T(8,128)(2,1)S(1)}, u32[]{:S(2)}, u32[]{:S(2)}) %collective-permute-start.10) | collective-permute-done | bytes 1310752 | tf_op jit(solution)/shard_map/ppermute | solution.py:17
  100.1 2.1 %slice_add_fusion = f32[256,2560]{1,0:T(8,128)S(1)} fusion(f32[512,2560]{1,0:T(8,128)} %fusion.4, bf16[256,2560]{1,0:T(8,128)(2,1)S(1)} %collective-permute-done.10), kind=kLoop, calls=%fused_computation.1 | loop fusion | flops 1310720 | bytes 6553600 | tf_op jit(solution)/shard_map/add | solution.py:316
  102.2 2.1 %collective-permute-start.11 = (bf16[128,2560]{1,0:T(8,128)(2,1)S(1)}, bf16[128,2560]{1,0:T(8,128)(2,1)S(1)}, u32[]{:S(2)}, u32[]{:S(2)}) collective-permute-start(bf16[128,2560]{1,0:T(8,128)(2,1)S(1)} %slice.98), channel_id=1, source_target_pairs={{0,2},{1,5},{2,0},{3,7},{4,6},{5,1},{6,4},{7,3},{8,10},{9,13},{10,... | collective-permute-start | bytes 1966088 | tf_op jit(solution)/shard_map/ppermute | solution.py:37
  104.3 8.6 %collective-permute-done.11 = bf16[128,2560]{1,0:T(8,128)(2,1)S(1)} collective-permute-done((bf16[128,2560]{1,0:T(8,128)(2,1)S(1)}, bf16[128,2560]{1,0:T(8,128)(2,1)S(1)}, u32[]{:S(2)}, u32[]{:S(2)}) %collective-permute-start.11) | collective-permute-done | bytes 655392 | tf_op jit(solution)/shard_map/ppermute | solution.py:37
  113.1 2.1 %collective-permute-start.12 = (bf16[64,2560]{1,0:T(8,128)(2,1)S(1)}, bf16[64,2560]{1,0:T(8,128)(2,1)S(1)}, u32[]{:S(2)}, u32[]{:S(2)}) collective-permute-start(bf16[64,2560]{1,0:T(8,128)(2,1)S(1)} %slice.99), channel_id=1, source_target_pairs={{0,4},{1,3},{2,6},{3,1},{4,0},{5,7},{6,2},{7,5},{8,12},{9,11},{10,... | collective-permute-start | bytes 983048 | tf_op jit(solution)/shard_map/ppermute | solution.py:37
  115.2 5.1 %collective-permute-done.12 = bf16[64,2560]{1,0:T(8,128)(2,1)S(1)} collective-permute-done((bf16[64,2560]{1,0:T(8,128)(2,1)S(1)}, bf16[64,2560]{1,0:T(8,128)(2,1)S(1)}, u32[]{:S(2)}, u32[]{:S(2)}) %collective-permute-start.12) | collective-permute-done | bytes 327712 | tf_op jit(solution)/shard_map/ppermute | solution.py:37
  120.4 2.3 %collective-permute-start.13 = (bf16[32,2560]{1,0:T(8,128)(2,1)S(1)}, bf16[32,2560]{1,0:T(8,128)(2,1)S(1)}, u32[]{:S(2)}, u32[]{:S(2)}) collective-permute-start(bf16[32,2560]{1,0:T(8,128)(2,1)S(1)} %slice.100), channel_id=1, source_target_pairs={{0,8},{1,17},{2,10},{3,19},{4,12},{5,21},{6,14},{7,23},{8,0},{9,25... | collective-permute-start | bytes 491528 | tf_op jit(solution)/shard_map/ppermute | solution.py:37
  122.6 4.1 %collective-permute-done.13 = bf16[32,2560]{1,0:T(8,128)(2,1)S(1)} collective-permute-done((bf16[32,2560]{1,0:T(8,128)(2,1)S(1)}, bf16[32,2560]{1,0:T(8,128)(2,1)S(1)}, u32[]{:S(2)}, u32[]{:S(2)}) %collective-permute-start.13) | collective-permute-done | bytes 163872 | tf_op jit(solution)/shard_map/ppermute | solution.py:37
  126.7 3.5 %collective-permute-start.14 = (bf16[16,2560]{1,0:T(8,128)(2,1)S(1)}, bf16[16,2560]{1,0:T(8,128)(2,1)S(1)}, u32[]{:S(2)}, u32[]{:S(2)}) collective-permute-start(bf16[16,2560]{1,0:T(8,128)(2,1)S(1)} %slice.101), channel_id=1, source_target_pairs={{0,16},{1,9},{2,18},{3,11},{4,20},{5,13},{6,22},{7,15},{8,24},{9,1... | collective-permute-start | bytes 245768 | tf_op jit(solution)/shard_map/ppermute | solution.py:37
  130.2 2.4 %collective-permute-done.14 = bf16[16,2560]{1,0:T(8,128)(2,1)S(1)} collective-permute-done((bf16[16,2560]{1,0:T(8,128)(2,1)S(1)}, bf16[16,2560]{1,0:T(8,128)(2,1)S(1)}, u32[]{:S(2)}, u32[]{:S(2)}) %collective-permute-start.14) | collective-permute-done | bytes 81952 | tf_op jit(solution)/shard_map/ppermute | solution.py:37
  (52 shorter events, 20.4 us)
Async XLA Ops:
  0.0 86.9 %copy-start = (bf16[512,2560]{1,0:T(8,128)(2,1)S(1)}, bf16[512,2560]{1,0:T(8,128)(2,1)}, u32[]{:S(2)}) copy-start(bf16[512,2560]{1,0:T(8,128)(2,1)} %param.18) | copy-start | bytes 7864324
  0.0 21.7 %copy-start.7 = (f32[2560]{0:T(1024)S(1)}, f32[2560]{0:T(1024)}, u32[]{:S(2)}) copy-start(f32[2560]{0:T(1024)} %param.13) | copy-start | bytes 30724
  0.0 30.0 %copy-start.8 = (s32[16,6]{0,1:T(8,128)S(1)}, s32[16,6]{0,1:T(8,128)}, u32[]{:S(2)}) copy-start(s32[16,6]{0,1:T(8,128)} %param.15) | copy-start | bytes 1156
  0.0 30.0 %copy-start.9 = (s32[16,6]{0,1:T(8,128)S(1)}, s32[16,6]{0,1:T(8,128)}, u32[]{:S(2)}) copy-start(s32[16,6]{0,1:T(8,128)} %param.14) | copy-start | bytes 1156
  0.0 3.1 %collective-permute-start.1 = (bf16[128,2560]{1,0:T(8,128)(2,1)}, bf16[128,2560]{1,0:T(8,128)(2,1)S(1)}, u32[]{:S(2)}, u32[]{:S(2)}) collective-permute-start(bf16[128,2560]{1,0:T(8,128)(2,1)} %values_a_ref.1), channel_id=1, source_target_pairs={{0,1},{1,0},{2,3},{3,2},{4,5},{5,4},{6,7},{7,6},{8,9},{9,8},{10,11... | collective-permute-start | bytes 1966088 | tf_op jit(solution)/shard_map/ppermute | solution.py:17
  0.6 2.5 %collective-permute-start = (bf16[128,1152]{1,0:T(8,128)(2,1)}, bf16[128,1152]{1,0:T(8,128)(2,1)}, u32[]{:S(2)}, u32[]{:S(2)}) collective-permute-start(bf16[128,1152]{1,0:T(8,128)(2,1)} %keys_a_ref.1), channel_id=1, source_target_pairs={{0,1},{1,0},{2,3},{3,2},{4,5},{5,4},{6,7},{7,6},{8,9},{9,8},{10,11... | collective-permute-start | bytes 884744 | tf_op jit(solution)/shard_map/ppermute | solution.py:17
  3.1 0.9 copy-start.1
  8.2 8.3 %collective-permute-start.2 = (bf16[64,2688]{1,0:T(8,128)(2,1)}, bf16[64,2688]{1,0:T(8,128)(2,1)S(1)}, u32[]{:S(2)}, u32[]{:S(2)}) collective-permute-start(bf16[64,2688]{1,0:T(8,128)(2,1)} %get-tuple-element.14), channel_id=1, source_target_pairs={{0,2},{1,5},{2,0},{3,7},{4,6},{5,1},{6,4},{7,3},{8,10},{9,13},{10,... | collective-permute-start | bytes 1032200 | tf_op jit(solution)/shard_map/ppermute | solution.py:37
  16.5 0.7 copy-start.2
  19.6 5.6 %collective-permute-start.3 = (bf16[32,2688]{1,0:T(8,128)(2,1)}, bf16[32,2688]{1,0:T(8,128)(2,1)S(1)}, u32[]{:S(2)}, u32[]{:S(2)}) collective-permute-start(bf16[32,2688]{1,0:T(8,128)(2,1)} %get-tuple-element.16), channel_id=1, source_target_pairs={{0,4},{1,9},{2,6},{3,11},{4,0},{5,13},{6,2},{7,15},{8,12},{9,1},{1... | collective-permute-start | bytes 516104 | tf_op jit(solution)/shard_map/ppermute | solution.py:37
  25.3 0.7 copy-start.3
  27.9 4.8 %collective-permute-start.4 = (bf16[16,2688]{1,0:T(8,128)(2,1)}, bf16[16,2688]{1,0:T(8,128)(2,1)S(1)}, u32[]{:S(2)}, u32[]{:S(2)}) collective-permute-start(bf16[16,2688]{1,0:T(8,128)(2,1)} %get-tuple-element.18), channel_id=1, source_target_pairs={{0,8},{1,3},{2,10},{3,1},{4,12},{5,7},{6,14},{7,5},{8,0},{9,11},{1... | collective-permute-start | bytes 258056 | tf_op jit(solution)/shard_map/ppermute | solution.py:37
  32.7 0.6 copy-start.4
  35.3 5.7 %collective-permute-start.5 = (bf16[16,2688]{1,0:T(8,128)(2,1)}, bf16[16,2688]{1,0:T(8,128)(2,1)S(1)}, u32[]{:S(2)}, u32[]{:S(2)}) collective-permute-start(bf16[16,2688]{1,0:T(8,128)(2,1)} %get-tuple-element.20), channel_id=1, source_target_pairs={{0,16},{1,9},{2,18},{3,11},{4,20},{5,13},{6,22},{7,15},{8,24},{9,1... | collective-permute-start | bytes 258056 | tf_op jit(solution)/shard_map/ppermute | solution.py:37
  41.9 8.2 %collective-permute-start.6 = (bf16[32,2688]{1,0:T(8,128)(2,1)S(1)}, bf16[32,2688]{1,0:T(8,128)(2,1)S(1)}, u32[]{:S(2)}, u32[]{:S(2)}) collective-permute-start(bf16[32,2688]{1,0:T(8,128)(2,1)S(1)} %pad_maximum_fusion.2), channel_id=1, source_target_pairs={{0,8},{1,17},{2,10},{3,19},{4,12},{5,21},{6,14},{7,23},{8,0},{9,25... | collective-permute-start | bytes 516104 | tf_op jit(solution)/shard_map/ppermute | solution.py:37
  51.0 9.8 %collective-permute-start.7 = (bf16[64,2688]{1,0:T(8,128)(2,1)S(1)}, bf16[64,2688]{1,0:T(8,128)(2,1)S(1)}, u32[]{:S(2)}, u32[]{:S(2)}) collective-permute-start(bf16[64,2688]{1,0:T(8,128)(2,1)S(1)} %pad_maximum_fusion.1), channel_id=1, source_target_pairs={{0,4},{1,3},{2,6},{3,1},{4,0},{5,7},{6,2},{7,5},{8,12},{9,11},{10,... | collective-permute-start | bytes 1032200 | tf_op jit(solution)/shard_map/ppermute | solution.py:37
  61.7 11.3 %collective-permute-start.8 = (bf16[128,2688]{1,0:T(8,128)(2,1)S(1)}, bf16[128,2688]{1,0:T(8,128)(2,1)S(1)}, u32[]{:S(2)}, u32[]{:S(2)}) collective-permute-start(bf16[128,2688]{1,0:T(8,128)(2,1)S(1)} %pad_maximum_fusion), channel_id=1, source_target_pairs={{0,2},{1,5},{2,0},{3,7},{4,6},{5,1},{6,4},{7,3},{8,10},{9,13},{10,... | collective-permute-start | bytes 2064392 | tf_op jit(solution)/shard_map/ppermute | solution.py:37
  73.9 1.5 %copy-start.6 = (bf16[512,2688]{1,0:T(8,128)(2,1)}, bf16[512,2688]{1,0:T(8,128)(2,1)S(1)}, u32[]{:S(2)}) copy-start(bf16[512,2688]{1,0:T(8,128)(2,1)S(1)} %get-tuple-element.24) | copy-start | bytes 8257540
  75.5 3.5 %collective-permute-start.9 = (bf16[256,2688]{1,0:T(8,128)(2,1)}, bf16[256,2688]{1,0:T(8,128)(2,1)}, u32[]{:S(2)}, u32[]{:S(2)}) collective-permute-start(bf16[256,2688]{1,0:T(8,128)(2,1)} %get-tuple-element.23), channel_id=1, source_target_pairs={{0,1},{1,0},{2,3},{3,2},{4,5},{5,4},{6,7},{7,6},{8,9},{9,8},{10,11... | collective-permute-start | bytes 4128776 | tf_op jit(solution)/shard_map/ppermute | solution.py:17
  75.5 6.0 %copy-start.10 = (bf16[512,2560]{1,0:T(8,128)(2,1)S(1)}, bf16[512,2560]{1,0:T(8,128)(2,1)}, u32[]{:S(2)}) copy-start(bf16[512,2560]{1,0:T(8,128)(2,1)} %param.17) | copy-start | bytes 7864324
  97.0 3.1 %collective-permute-start.10 = (bf16[256,2560]{1,0:T(8,128)(2,1)S(1)}, bf16[256,2560]{1,0:T(8,128)(2,1)S(1)}, u32[]{:S(2)}, u32[]{:S(2)}) collective-permute-start(bf16[256,2560]{1,0:T(8,128)(2,1)S(1)} %slice.97), channel_id=1, source_target_pairs={{0,1},{1,0},{2,3},{3,2},{4,5},{5,4},{6,7},{7,6},{8,9},{9,8},{10,11... | collective-permute-start | bytes 3932168 | tf_op jit(solution)/shard_map/ppermute | solution.py:17
  102.2 10.7 %collective-permute-start.11 = (bf16[128,2560]{1,0:T(8,128)(2,1)S(1)}, bf16[128,2560]{1,0:T(8,128)(2,1)S(1)}, u32[]{:S(2)}, u32[]{:S(2)}) collective-permute-start(bf16[128,2560]{1,0:T(8,128)(2,1)S(1)} %slice.98), channel_id=1, source_target_pairs={{0,2},{1,5},{2,0},{3,7},{4,6},{5,1},{6,4},{7,3},{8,10},{9,13},{10,... | collective-permute-start | bytes 1966088 | tf_op jit(solution)/shard_map/ppermute | solution.py:37
  113.1 19.6 %copy-start.5 = (bf16[16,2560]{1,0:T(8,128)(2,1)S(1)}, bf16[16,2560]{1,0:T(8,128)(2,1)}, u32[]{:S(2)}) copy-start(bf16[16,2560]{1,0:T(8,128)(2,1)} %get-tuple-element.19) | copy-start | bytes 245764
  113.1 7.1 %collective-permute-start.12 = (bf16[64,2560]{1,0:T(8,128)(2,1)S(1)}, bf16[64,2560]{1,0:T(8,128)(2,1)S(1)}, u32[]{:S(2)}, u32[]{:S(2)}) collective-permute-start(bf16[64,2560]{1,0:T(8,128)(2,1)S(1)} %slice.99), channel_id=1, source_target_pairs={{0,4},{1,3},{2,6},{3,1},{4,0},{5,7},{6,2},{7,5},{8,12},{9,11},{10,... | collective-permute-start | bytes 983048 | tf_op jit(solution)/shard_map/ppermute | solution.py:37
  120.4 6.3 %collective-permute-start.13 = (bf16[32,2560]{1,0:T(8,128)(2,1)S(1)}, bf16[32,2560]{1,0:T(8,128)(2,1)S(1)}, u32[]{:S(2)}, u32[]{:S(2)}) collective-permute-start(bf16[32,2560]{1,0:T(8,128)(2,1)S(1)} %slice.100), channel_id=1, source_target_pairs={{0,8},{1,17},{2,10},{3,19},{4,12},{5,21},{6,14},{7,23},{8,0},{9,25... | collective-permute-start | bytes 491528 | tf_op jit(solution)/shard_map/ppermute | solution.py:37
  126.7 5.9 %collective-permute-start.14 = (bf16[16,2560]{1,0:T(8,128)(2,1)S(1)}, bf16[16,2560]{1,0:T(8,128)(2,1)S(1)}, u32[]{:S(2)}, u32[]{:S(2)}) collective-permute-start(bf16[16,2560]{1,0:T(8,128)(2,1)S(1)} %slice.101), channel_id=1, source_target_pairs={{0,16},{1,9},{2,18},{3,11},{4,20},{5,13},{6,22},{7,15},{8,24},{9,1... | collective-permute-start | bytes 245768 | tf_op jit(solution)/shard_map/ppermute | solution.py:37

commit v3 on v2

--- a/solution.py
+++ b/solution.py
@@ -7,8 +7,21 @@
 from jax.experimental.pallas import tpu as pltpu
 from jax.sharding import PartitionSpec as P
 
+
 HEADS = 16
 LANES = 128
+
+
+def near(value):
+    return pltpu.with_memory_space_constraint(value, pltpu.VMEM)
+
+
+def far(value):
+    return pltpu.with_memory_space_constraint(value, pltpu.HBM)
+
+
+def near_shape(shape, dtype):
+    return pltpu.VMEM(shape, dtype)
 
 
 def partner(value, axis, stride):
@@ -212,7 +225,74 @@
     block_ref[:, model_width:] = table_ref[...]
 
 
-def attention_rows(queries, patch_keys, patch_values, norm_gain, table, row_count):
+def expert_kernel(
+    steps, expert_ref, rows_ref, gate_a, gate_b, up_a, up_b, down_a, down_b, out_ref, total_ref
+):
+    step = pl.program_id(0)
+    model_width = total_ref.shape[1]
+    contract_last = (((1,), (1,)), ((), ()))
+
+    def add_units(gate_ref, up_ref, down_ref):
+        rows = rows_ref[:, :model_width]
+        scores = rows_ref[:, model_width:].astype(jnp.float32)
+        chosen = jnp.where(lane_iota(scores.shape) == expert_ref[0], scores, 0.0)
+        share = jnp.sum(chosen, axis=1, keepdims=True) / jnp.sum(scores, axis=1, keepdims=True)
+        gate_part = lax.dot_general(
+            rows, gate_ref[...], contract_last, preferred_element_type=jnp.float32
+        )
+        up_part = lax.dot_general(
+            rows, up_ref[...], contract_last, preferred_element_type=jnp.float32
+        )
+        silu = gate_part / (1.0 + jnp.exp(-gate_part))
+        hidden = (silu * up_part * share).astype(jnp.bfloat16)
+        total_ref[...] += jnp.dot(hidden, down_ref[...], preferred_element_type=jnp.float32)
+
+    @pl.when(step == 0)
+    def _():
+        total_ref[...] = jnp.zeros_like(total_ref)
+
+    @pl.when(step < steps)
+    def _():
+        add_units(gate_a, up_a, down_a)
+
+    @pl.when(step >= steps)
+    def _():
+        add_units(gate_b, up_b, down_b)
+
+    @pl.when(step == 2 * steps - 1)
+    def _():
+        out_ref[...] = total_ref[...].astype(out_ref.dtype)
+
+
+def expert_rows(expert, rows, weights, out_dtype):
+    units, model_width = weights[0].shape
+    row_count = rows.shape[0]
+    whole = pl.BlockSpec(memory_space=pltpu.VMEM)
+    tile = min(2 * LANES, units)
+    steps = units // tile
+    first = pl.BlockSpec((tile, model_width), lambda step: (jnp.minimum(step, steps - 1), 0))
+    second = pl.BlockSpec((tile, model_width), lambda step: (jnp.maximum(step - steps, 0), 0))
+    flops = 2 * 3 * row_count * model_width * units * 2
+    return pl.pallas_call(
+        functools.partial(expert_kernel, steps),
+        name="expert",
+        grid=(2 * steps,),
+        compiler_params=pltpu.CompilerParams(vmem_limit_bytes=36 << 20),
+        out_shape=near_shape((row_count, model_width), out_dtype),
+        in_specs=[pl.BlockSpec(memory_space=pltpu.SMEM), whole] + [first, second] * 3,
+        out_specs=whole,
+        scratch_shapes=[pltpu.VMEM((row_count, model_width), jnp.float32)],
+        cost_estimate=pl.CostEstimate(
+            flops=flops,
+            transcendentals=0,
+            bytes_accessed=12 * units * model_width,
+        ),
+    )(expert, near(rows), *[far(weight) for weight in weights])
+
+
+def attention_rows(
+    queries, patch_keys, patch_values, other_keys, other_values, norm_gain, table, row_count
+):
     model_width = patch_values.shape[1]
     packed_width = model_width + LANES
     group_size = queries.shape[0] // row_count
@@ -233,54 +313,60 @@
     masks = jnp.array(masks, jnp.int32)
     blocks = (device_index % group_size) ^ jnp.where(device_index % 2 == 1, masks[1], masks[0])
     rows = row_count << stages
-    other_keys = partner(patch_keys, "wide", 0)
-    other_values = partner(patch_values, "wide", 0)
     whole = pl.BlockSpec(memory_space=pltpu.VMEM)
 
     def pair_shapes(rows):
         return (
-            jax.ShapeDtypeStruct((rows, packed_width), jnp.bfloat16),
-            jax.ShapeDtypeStruct((rows, packed_width), jnp.float32),
+            near_shape((rows, packed_width), jnp.bfloat16),
+            near_shape((rows, packed_width), jnp.float32),
         )
 
     sent, kept = pl.pallas_call(
         functools.partial(attend_kernel, HEADS, row_count),
         name="attend",
+        compiler_params=pltpu.CompilerParams(vmem_limit_bytes=12 << 20),
         out_shape=pair_shapes(rows // 2),
         in_specs=[pl.BlockSpec(memory_space=pltpu.SMEM)] + [whole] * 5,
         out_specs=(whole, whole),
         scratch_shapes=[pltpu.VMEM((rows, queries.shape[1]), jnp.bfloat16)],
-    )(blocks, queries, patch_keys, other_keys, patch_values, other_values)
+    )(
+        blocks,
+        far(queries),
+        far(patch_keys),
+        near(other_keys),
+        far(patch_values),
+        near(other_values),
+    )
     for stage in range(stages - 1):
         came = exchange(sent, orders, stage)
         sent, kept = pl.pallas_call(
             functools.partial(merge_kernel, HEADS),
             name="merge",
+            compiler_params=pltpu.CompilerParams(vmem_limit_bytes=6 << 20),
             out_shape=pair_shapes(kept.shape[0] // 2),
             in_specs=[whole] * 2,
             out_specs=(whole, whole),
-        )(kept, came)
+        )(near(kept), near(came))
     came = exchange(sent, orders, stages - 1)
     return pl.pallas_call(
         functools.partial(finish_kernel, HEADS),
         name="finish",
+        compiler_params=pltpu.CompilerParams(vmem_limit_bytes=6 << 20),
         out_shape=(
-            jax.ShapeDtypeStruct((row_count, packed_width), jnp.bfloat16),
-            jax.ShapeDtypeStruct((row_count, model_width), jnp.bfloat16),
+            near_shape((row_count, packed_width), jnp.bfloat16),
+            near_shape((row_count, model_width), jnp.bfloat16),
         ),
         in_specs=[whole] * 4,
         out_specs=(whole, whole),
-    )(kept, came, norm_gain.reshape(1, model_width), table)
+    )(near(kept), near(came), near(norm_gain.reshape(1, model_width)), near(table))
 
 
 def on_device(
     queries, patch_keys, patch_values, norm_gain, route_experts, route_weights, w_gate, w_up, w_down
 ):
     row_count = route_experts.shape[0]
-    model_width = patch_values.shape[1]
     devices = lax.axis_size("wide")
     device_index = lax.axis_index("wide")
-    experts = devices // 2
     score_table = jnp.sum(
         jnp.where(
             route_experts[:, :, None] == jnp.arange(LANES, dtype=jnp.int32)[None, None, :],
@@ -289,34 +375,34 @@
         ),
         axis=1,
     ).astype(jnp.bfloat16)
+    other_keys = partner(patch_keys, "wide", 0)
+    other_values = partner(patch_values, "wide", 0)
+    halves, other_keys, other_values = lax.optimization_barrier(
+        ((w_gate, w_up, w_down), other_keys, other_values)
+    )
+    weights = []
+    for own in halves:
+        weights += [own, partner(own, "wide", 0)]
     block, projected = attention_rows(
-        queries, patch_keys, patch_values, norm_gain, score_table, row_count
+        queries,
+        patch_keys,
+        patch_values,
+        other_keys,
+        other_values,
+        norm_gain,
+        score_table,
+        row_count,
     )
     orders = stage_orders(devices)
-    for stage in range(len(orders[0])):
+    stages = len(orders[0])
+    for stage in range(stages - 1):
         block = jnp.concatenate([block, exchange(block, orders, stage)], axis=0)
-    block = jnp.concatenate([block, partner(block, "wide", 0)], axis=0)
-    rows_in = block[:, :model_width]
-    score_rows = block[:, model_width : model_width + experts].astype(jnp.float32)
-    own_expert = jnp.arange(experts, dtype=jnp.int32)[None, :] == device_index // 2
-    share = jnp.sum(jnp.where(own_expert, score_rows, 0.0), axis=1, keepdims=True) / jnp.sum(
-        score_rows, axis=1, keepdims=True
-    )
-    gate_part = lax.dot_general(
-        rows_in, w_gate, (((1,), (1,)), ((), ())), preferred_element_type=jnp.float32
-    )
-    up_part = lax.dot_general(
-        rows_in, w_up, (((1,), (1,)), ((), ())), preferred_element_type=jnp.float32
-    )
-    hidden = (jax.nn.silu(gate_part) * up_part * share).astype(jnp.bfloat16)
-    partial_value = lax.dot_general(
-        hidden, w_down, (((1,), (0,)), ((), ())), preferred_element_type=jnp.float32
-    )
-    half_rows = partial_value.shape[0] // 2
-    total = partial_value[:half_rows] + partner(
-        partial_value[half_rows:].astype(jnp.bfloat16), "wide", 0
-    ).astype(jnp.float32)
-    for stage in reversed(range(len(orders[0]))):
+    came = exchange(block, orders, stages - 1)
+    expert = (device_index // 2).reshape(1)
+    total = expert_rows(expert, block, weights, jnp.float32)
+    sent = expert_rows(expert, came, weights, jnp.bfloat16)
+    total = total + exchange(sent, orders, stages - 1).astype(jnp.float32)
+    for stage in reversed(range(stages - 1)):
         half_rows = total.shape[0] // 2
         total = total[:half_rows] + exchange(
             total[half_rows:].astype(jnp.bfloat16), orders, stage
@@ -325,6 +411,10 @@
 
 
 def solution(mesh):
+    return mapped(mesh)
+
+
+def mapped(mesh):
     return jax.shard_map(
         on_device,
         mesh=mesh,

time: 134 us -> 104 us (0.78)
  local copies, waits for them, and re-layouts: 14.2 us -> 0.16 us
  matrix products: 12.5 us -> 0 us
  Pallas kernels: 10.6 us -> 22.9 us
  waiting for transfers between devices: 56.9 us -> 45.3 us
  other arithmetic: 8.76 us -> 1.73 us
  starting transfers between devices: 30.2 us -> 33.8 us
    pallas_call x3 -> x5, Pallas kernels: 6.34 us -> 19.9 us  [the longest x2 18.9 us: expert_rows(): pl.pallas_call(functools.partial(expert_kernel, steps), name='expert', gr...]
    dot_general x2 -> x0, matrix products: 12.5 us -> none  [the longest x1 8.2 us: on_device(): lax.dot_general(hidden, w_down, (((1,), (0,)), ((), ())), preferred_eleme...]
    unnamed x26 -> x9, local copies, waits for them, and re-layouts: 8.11 us -> 0.05 us
    ppermute x4 -> x5, waiting for transfers between devices: 7.52 us -> 1.62 us  [partner(): return lax.ppermute(value, axis, pairs)]
    ppermute x11, waiting for transfers between devices: 49.4 us -> 43.7 us  [exchange(): return lax.ppermute(value, 'wide', pairs)]
    ppermute x11, starting transfers between devices: 29.4 us -> 32.6 us  [exchange(): return lax.ppermute(value, 'wide', pairs)]
    concatenate x3 -> x2, other arithmetic: 2.75 us -> 0.05 us  [on_device(): block = jnp.concatenate([block, exchange(block, orders, stage)], axis=0)]
    concatenate x1 -> x0, local copies, waits for them, and re-layouts: 2.53 us -> none  [on_device(): block = jnp.concatenate([block, partner(block, 'wide', 0)], axis=0)]
  transfers between devices with their start and end apart: 15 -> 16, of which waited for: 14 -> 12; matrix products, arithmetic and copies ran while one was open for 5% -> 1% of each run, Pallas kernels for 0% -> 9%
where the time goes in v3:
time: 104 us
  waiting for transfers between devices  45.3 us (44%)
  starting transfers between devices  33.8 us (32%)
  Pallas kernels  22.9 us (22%)
  other arithmetic  1.73 us (2%)
    ppermute x11, waiting for transfers between devices, exchange(): return lax.ppermute(value, 'wide', pairs)  43.7 us
    ppermute x11, starting transfers between devices, exchange(): return lax.ppermute(value, 'wide', pairs)  32.6 us
    pallas_call x2, Pallas kernels, expert_rows(): pl.pallas_call(functools.partial(expert_kernel, steps), name='expert', gr...  18.9 us
    pallas_call x1, Pallas kernels, attention_rows(): pl.pallas_call(functools.partial(attend_kernel, HEADS, row_count), name='...  3 us
  transfers between devices with their start and end apart: 16, of which 12 were waited for; matrix products, arithmetic and copies ran while one was open for 1% of the time, Pallas kernels for 9%

profile of v3, /device:TPU:0, one launch (start us, length us, event | category | flops | bytes accessed | tf_op | source)
XLA Modules:
  0.0 104.0 jit_solution(18217614414746526068)
XLA Ops:
  0.0 0.6 collective-permute-start.1
  0.6 0.7 fusion.3.blocks_ref
  1.3 1.6 %collective-permute-done.keys_b_ref = bf16[128,1152]{1,0:T(8,128)(2,1)S(1)} collective-permute-done((bf16[128,1152]{1,0:T(8,128)(2,1)}, bf16[128,1152]{1,0:T(8,128)(2,1)S(1)}, u32[]{:S(2)}, u32[]{:S(2)}) %collective-permute-start) | collective-permute-done | bytes 294944 | tf_op jit(solution)/shard_map/ppermute | solution.py:30
  2.9 3.0 %attend.1 = (bf16[64,2688]{1,0:T(8,128)(2,1)S(1)}, f32[64,2688]{1,0:T(8,128)S(1)}) custom-call(s32[8]{0:T(128)S(1)} %fusion.3.blocks_ref, bf16[256,1152]{1,0:T(8,128)(2,1)} %queries_ref.1, bf16[128,1152]{1,0:T(8,128)(2,1)} %keys_a_ref.1, bf16[128,1152]{1,0:T(8,128)(2,1)S(1)} %collective-permute-done.keys_b_ref, bf16[128,2560]{1,0:T(8,128)(2,1)} %values_a_ref.1, ...), custom_call_target="tpu_custom_call" | custom-call | tf_op jit(solution)/shard_map/attend/pallas_call | solution.py:324
  5.9 2.9 %collective-permute-start.2 = (bf16[64,2688]{1,0:T(8,128)(2,1)S(1)}, bf16[64,2688]{1,0:T(8,128)(2,1)S(1)}, u32[]{:S(2)}, u32[]{:S(2)}) collective-permute-start(bf16[64,2688]{1,0:T(8,128)(2,1)S(1)} %get-tuple-element.21), channel_id=1, source_target_pairs={{0,2},{1,5},{2,0},{3,7},{4,6},{5,1},{6,4},{7,3},{8,10},{9,13},{10,... | collective-permute-start | bytes 1032200 | tf_op jit(solution)/shard_map/ppermute | solution.py:50
  8.8 5.2 %collective-permute-done.2.came_ref = bf16[64,2688]{1,0:T(8,128)(2,1)S(1)} collective-permute-done((bf16[64,2688]{1,0:T(8,128)(2,1)S(1)}, bf16[64,2688]{1,0:T(8,128)(2,1)S(1)}, u32[]{:S(2)}, u32[]{:S(2)}) %collective-permute-start.2) | collective-permute-done | bytes 344096 | tf_op jit(solution)/shard_map/ppermute | solution.py:50
  14.1 0.4 merge.2
  14.5 2.1 %collective-permute-start.3 = (bf16[32,2688]{1,0:T(8,128)(2,1)S(1)}, bf16[32,2688]{1,0:T(8,128)(2,1)S(1)}, u32[]{:S(2)}, u32[]{:S(2)}) collective-permute-start(bf16[32,2688]{1,0:T(8,128)(2,1)S(1)} %get-tuple-element.23), channel_id=1, source_target_pairs={{0,4},{1,9},{2,6},{3,11},{4,0},{5,13},{6,2},{7,15},{8,12},{9,1},{1... | collective-permute-start | bytes 516104 | tf_op jit(solution)/shard_map/ppermute | solution.py:50
  16.6 3.4 %collective-permute-done.3.came_ref = bf16[32,2688]{1,0:T(8,128)(2,1)S(1)} collective-permute-done((bf16[32,2688]{1,0:T(8,128)(2,1)S(1)}, bf16[32,2688]{1,0:T(8,128)(2,1)S(1)}, u32[]{:S(2)}, u32[]{:S(2)}) %collective-permute-start.3) | collective-permute-done | bytes 172064 | tf_op jit(solution)/shard_map/ppermute | solution.py:50
  20.2 2.1 %collective-permute-start.4 = (bf16[16,2688]{1,0:T(8,128)(2,1)S(1)}, bf16[16,2688]{1,0:T(8,128)(2,1)S(1)}, u32[]{:S(2)}, u32[]{:S(2)}) collective-permute-start(bf16[16,2688]{1,0:T(8,128)(2,1)S(1)} %get-tuple-element.25), channel_id=1, source_target_pairs={{0,8},{1,3},{2,10},{3,1},{4,12},{5,7},{6,14},{7,5},{8,0},{9,11},{1... | collective-permute-start | bytes 258056 | tf_op jit(solution)/shard_map/ppermute | solution.py:50
  22.5 2.3 %collective-permute-done.4.came_ref = bf16[16,2688]{1,0:T(8,128)(2,1)S(1)} collective-permute-done((bf16[16,2688]{1,0:T(8,128)(2,1)S(1)}, bf16[16,2688]{1,0:T(8,128)(2,1)S(1)}, u32[]{:S(2)}, u32[]{:S(2)}) %collective-permute-start.4) | collective-permute-done | bytes 86048 | tf_op jit(solution)/shard_map/ppermute | solution.py:50
  24.8 0.4 finish.1
  25.2 3.1 %collective-permute-start.5 = (bf16[16,2688]{1,0:T(8,128)(2,1)S(1)}, bf16[16,2688]{1,0:T(8,128)(2,1)S(1)}, u32[]{:S(2)}, u32[]{:S(2)}) collective-permute-start(bf16[16,2688]{1,0:T(8,128)(2,1)S(1)} %get-tuple-element.27), channel_id=1, source_target_pairs={{0,16},{1,9},{2,18},{3,11},{4,20},{5,13},{6,22},{7,15},{8,24},{9,1... | collective-permute-start | bytes 258056 | tf_op jit(solution)/shard_map/ppermute | solution.py:50
  28.3 0.5 collective-permute-start.9
  28.8 2.0 %collective-permute-done.5 = bf16[16,2688]{1,0:T(8,128)(2,1)S(1)} collective-permute-done((bf16[16,2688]{1,0:T(8,128)(2,1)S(1)}, bf16[16,2688]{1,0:T(8,128)(2,1)S(1)}, u32[]{:S(2)}, u32[]{:S(2)}) %collective-permute-start.5) | collective-permute-done | bytes 86048 | tf_op jit(solution)/shard_map/ppermute | solution.py:50
  30.8 4.7 %collective-permute-start.6 = (bf16[32,2688]{1,0:T(8,128)(2,1)S(1)}, bf16[32,2688]{1,0:T(8,128)(2,1)S(1)}, u32[]{:S(2)}, u32[]{:S(2)}) collective-permute-start(bf16[32,2688]{1,0:T(8,128)(2,1)S(1)} %pad_maximum_fusion.1), channel_id=1, source_target_pairs={{0,8},{1,17},{2,10},{3,19},{4,12},{5,21},{6,14},{7,23},{8,0},{9,25... | collective-permute-start | bytes 516104 | tf_op jit(solution)/shard_map/ppermute | solution.py:50
  35.5 3.4 %collective-permute-done.6 = bf16[32,2688]{1,0:T(8,128)(2,1)S(1)} collective-permute-done((bf16[32,2688]{1,0:T(8,128)(2,1)S(1)}, bf16[32,2688]{1,0:T(8,128)(2,1)S(1)}, u32[]{:S(2)}, u32[]{:S(2)}) %collective-permute-start.6) | collective-permute-done | bytes 172064 | tf_op jit(solution)/shard_map/ppermute | solution.py:50
  38.9 1.6 %collective-permute-start.7 = (bf16[64,2688]{1,0:T(8,128)(2,1)S(1)}, bf16[64,2688]{1,0:T(8,128)(2,1)S(1)}, u32[]{:S(2)}, u32[]{:S(2)}) collective-permute-start(bf16[64,2688]{1,0:T(8,128)(2,1)S(1)} %pad_maximum_fusion), channel_id=1, source_target_pairs={{0,4},{1,3},{2,6},{3,1},{4,0},{5,7},{6,2},{7,5},{8,12},{9,11},{10,... | collective-permute-start | bytes 1032200 | tf_op jit(solution)/shard_map/ppermute | solution.py:50
  40.5 6.3 %collective-permute-done.7 = bf16[64,2688]{1,0:T(8,128)(2,1)S(1)} collective-permute-done((bf16[64,2688]{1,0:T(8,128)(2,1)S(1)}, bf16[64,2688]{1,0:T(8,128)(2,1)S(1)}, u32[]{:S(2)}, u32[]{:S(2)}) %collective-permute-start.7) | collective-permute-done | bytes 344096 | tf_op jit(solution)/shard_map/ppermute | solution.py:50
  46.9 1.5 %collective-permute-start.11 = (bf16[128,2688]{1,0:T(8,128)(2,1)S(1)}, bf16[128,2688]{1,0:T(8,128)(2,1)S(1)}, u32[]{:S(2)}, u32[]{:S(2)}) collective-permute-start(bf16[128,2688]{1,0:T(8,128)(2,1)S(1)} %constant_dynamic-update-slice_fusion.rows_ref), channel_id=1, source_target_pairs={{0,2},{1,5},{2,0},{3,7},{4,6},{5,1},{6,4},{7,3},{8,10},{9,13},{10,... | collective-permute-start | bytes 2064392 | tf_op jit(solution)/shard_map/ppermute | solution.py:50
  48.4 9.5 %collective-permute-done.11.rows_ref = bf16[128,2688]{1,0:T(8,128)(2,1)S(1)} collective-permute-done((bf16[128,2688]{1,0:T(8,128)(2,1)S(1)}, bf16[128,2688]{1,0:T(8,128)(2,1)S(1)}, u32[]{:S(2)}, u32[]{:S(2)}) %collective-permute-start.11) | collective-permute-done | bytes 688160 | tf_op jit(solution)/shard_map/ppermute | solution.py:50
  57.9 9.5 %expert.3 = bf16[128,2560]{1,0:T(8,128)(2,1)S(1)} custom-call(s32[1]{0:T(128)} %bitcast.1.expert_ref, bf16[128,2688]{1,0:T(8,128)(2,1)S(1)} %collective-permute-done.11.rows_ref, bf16[512,2560]{1,0:T(8,128)(2,1)} %gate_a.1, bf16[512,2560]{1,0:T(8,128)(2,1)} %collective-permute-done.8.gate_b, bf16[512,2560]{1,0:T(8,128)(2,1)} %up_a.1, ...), custom_call_target="tpu_custom_call" | custom-call | flops 2013265920 | bytes 15728640 | tf_op jit(solution)/shard_map/expert/pallas_call | solution.py:276
  67.4 1.6 %collective-permute-start.12 = (bf16[128,2560]{1,0:T(8,128)(2,1)S(1)}, bf16[128,2560]{1,0:T(8,128)(2,1)S(1)}, u32[]{:S(2)}, u32[]{:S(2)}) collective-permute-start(bf16[128,2560]{1,0:T(8,128)(2,1)S(1)} %expert.3), channel_id=1, source_target_pairs={{0,2},{1,5},{2,0},{3,7},{4,6},{5,1},{6,4},{7,3},{8,10},{9,13},{10,... | collective-permute-start | bytes 1966088 | tf_op jit(solution)/shard_map/ppermute | solution.py:50
  68.9 9.5 %expert.2 = f32[128,2560]{1,0:T(8,128)S(1)} custom-call(s32[1]{0:T(128)} %bitcast.1.expert_ref, bf16[128,2688]{1,0:T(8,128)(2,1)S(1)} %constant_dynamic-update-slice_fusion.rows_ref, bf16[512,2560]{1,0:T(8,128)(2,1)} %gate_a.1, bf16[512,2560]{1,0:T(8,128)(2,1)} %collective-permute-done.8.gate_b, bf16[512,2560]{1,0:T(8,128)(2,1)} %up_a.1, ...), custom_call_target="tpu_custom_call" | custom-call | flops 2013265920 | bytes 15728640 | tf_op jit(solution)/shard_map/expert/pallas_call | solution.py:276
  78.4 0.8 collective-permute-done.12
  79.4 2.6 %collective-permute-start.13 = (bf16[64,2560]{1,0:T(8,128)(2,1)S(1)}, bf16[64,2560]{1,0:T(8,128)(2,1)S(1)}, u32[]{:S(2)}, u32[]{:S(2)}) collective-permute-start(bf16[64,2560]{1,0:T(8,128)(2,1)S(1)} %slice.51), channel_id=1, source_target_pairs={{0,4},{1,3},{2,6},{3,1},{4,0},{5,7},{6,2},{7,5},{8,12},{9,11},{10,... | collective-permute-start | bytes 983048 | tf_op jit(solution)/shard_map/ppermute | solution.py:50
  82.0 5.1 %collective-permute-done.13 = bf16[64,2560]{1,0:T(8,128)(2,1)S(1)} collective-permute-done((bf16[64,2560]{1,0:T(8,128)(2,1)S(1)}, bf16[64,2560]{1,0:T(8,128)(2,1)S(1)}, u32[]{:S(2)}, u32[]{:S(2)}) %collective-permute-start.13) | collective-permute-done | bytes 327712 | tf_op jit(solution)/shard_map/ppermute | solution.py:50
  87.1 6.1 %collective-permute-start.14 = (bf16[32,2560]{1,0:T(8,128)(2,1)S(1)}, bf16[32,2560]{1,0:T(8,128)(2,1)S(1)}, u32[]{:S(2)}, u32[]{:S(2)}) collective-permute-start(bf16[32,2560]{1,0:T(8,128)(2,1)S(1)} %slice.52), channel_id=1, source_target_pairs={{0,8},{1,17},{2,10},{3,19},{4,12},{5,21},{6,14},{7,23},{8,0},{9,25... | collective-permute-start | bytes 491528 | tf_op jit(solution)/shard_map/ppermute | solution.py:50
  93.2 3.3 %collective-permute-done.14 = bf16[32,2560]{1,0:T(8,128)(2,1)S(1)} collective-permute-done((bf16[32,2560]{1,0:T(8,128)(2,1)S(1)}, bf16[32,2560]{1,0:T(8,128)(2,1)S(1)}, u32[]{:S(2)}, u32[]{:S(2)}) %collective-permute-start.14) | collective-permute-done | bytes 163872 | tf_op jit(solution)/shard_map/ppermute | solution.py:50
  96.6 4.3 %collective-permute-start.15 = (bf16[16,2560]{1,0:T(8,128)(2,1)S(1)}, bf16[16,2560]{1,0:T(8,128)(2,1)S(1)}, u32[]{:S(2)}, u32[]{:S(2)}) collective-permute-start(bf16[16,2560]{1,0:T(8,128)(2,1)S(1)} %slice.53), channel_id=1, source_target_pairs={{0,16},{1,9},{2,18},{3,11},{4,20},{5,13},{6,22},{7,15},{8,24},{9,1... | collective-permute-start | bytes 245768 | tf_op jit(solution)/shard_map/ppermute | solution.py:50
  100.9 2.4 %collective-permute-done.15 = bf16[16,2560]{1,0:T(8,128)(2,1)S(1)} collective-permute-done((bf16[16,2560]{1,0:T(8,128)(2,1)S(1)}, bf16[16,2560]{1,0:T(8,128)(2,1)S(1)}, u32[]{:S(2)}, u32[]{:S(2)}) %collective-permute-start.15) | collective-permute-done | bytes 81952 | tf_op jit(solution)/shard_map/ppermute | solution.py:50
  103.3 0.7 fusion.1
  (29 shorter events, 0.9 us)
Async XLA Ops:
  0.0 22.4 %copy-start.1 = (s32[16,6]{0,1:T(8,128)S(1)}, s32[16,6]{0,1:T(8,128)}, u32[]{:S(2)}) copy-start(s32[16,6]{0,1:T(8,128)} %param.15) | copy-start | bytes 1156
  0.0 22.4 %copy-start.2 = (s32[16,6]{0,1:T(8,128)S(1)}, s32[16,6]{0,1:T(8,128)}, u32[]{:S(2)}) copy-start(s32[16,6]{0,1:T(8,128)} %param.14) | copy-start | bytes 1156
  0.0 22.5 %copy-start = (f32[2560]{0:T(1024)S(1)}, f32[2560]{0:T(1024)}, u32[]{:S(2)}) copy-start(f32[2560]{0:T(1024)} %param.13) | copy-start | bytes 30724
  0.0 2.9 %collective-permute-start.1 = (bf16[128,2560]{1,0:T(8,128)(2,1)}, bf16[128,2560]{1,0:T(8,128)(2,1)S(1)}, u32[]{:S(2)}, u32[]{:S(2)}) collective-permute-start(bf16[128,2560]{1,0:T(8,128)(2,1)} %values_a_ref.1), channel_id=1, source_target_pairs={{0,1},{1,0},{2,3},{3,2},{4,5},{5,4},{6,7},{7,6},{8,9},{9,8},{10,11... | collective-permute-start | bytes 1966088 | tf_op jit(solution)/shard_map/ppermute | solution.py:30
  0.6 2.4 %collective-permute-start = (bf16[128,1152]{1,0:T(8,128)(2,1)}, bf16[128,1152]{1,0:T(8,128)(2,1)S(1)}, u32[]{:S(2)}, u32[]{:S(2)}) collective-permute-start(bf16[128,1152]{1,0:T(8,128)(2,1)} %keys_a_ref.1), channel_id=1, source_target_pairs={{0,1},{1,0},{2,3},{3,2},{4,5},{5,4},{6,7},{7,6},{8,9},{9,8},{10,11... | collective-permute-start | bytes 884744 | tf_op jit(solution)/shard_map/ppermute | solution.py:30
  5.9 8.1 %collective-permute-start.2 = (bf16[64,2688]{1,0:T(8,128)(2,1)S(1)}, bf16[64,2688]{1,0:T(8,128)(2,1)S(1)}, u32[]{:S(2)}, u32[]{:S(2)}) collective-permute-start(bf16[64,2688]{1,0:T(8,128)(2,1)S(1)} %get-tuple-element.21), channel_id=1, source_target_pairs={{0,2},{1,5},{2,0},{3,7},{4,6},{5,1},{6,4},{7,3},{8,10},{9,13},{10,... | collective-permute-start | bytes 1032200 | tf_op jit(solution)/shard_map/ppermute | solution.py:50
  14.5 5.5 %collective-permute-start.3 = (bf16[32,2688]{1,0:T(8,128)(2,1)S(1)}, bf16[32,2688]{1,0:T(8,128)(2,1)S(1)}, u32[]{:S(2)}, u32[]{:S(2)}) collective-permute-start(bf16[32,2688]{1,0:T(8,128)(2,1)S(1)} %get-tuple-element.23), channel_id=1, source_target_pairs={{0,4},{1,9},{2,6},{3,11},{4,0},{5,13},{6,2},{7,15},{8,12},{9,1},{1... | collective-permute-start | bytes 516104 | tf_op jit(solution)/shard_map/ppermute | solution.py:50
  20.2 4.6 %collective-permute-start.4 = (bf16[16,2688]{1,0:T(8,128)(2,1)S(1)}, bf16[16,2688]{1,0:T(8,128)(2,1)S(1)}, u32[]{:S(2)}, u32[]{:S(2)}) collective-permute-start(bf16[16,2688]{1,0:T(8,128)(2,1)S(1)} %get-tuple-element.25), channel_id=1, source_target_pairs={{0,8},{1,3},{2,10},{3,1},{4,12},{5,7},{6,14},{7,5},{8,0},{9,11},{1... | collective-permute-start | bytes 258056 | tf_op jit(solution)/shard_map/ppermute | solution.py:50
  25.2 5.6 %collective-permute-start.5 = (bf16[16,2688]{1,0:T(8,128)(2,1)S(1)}, bf16[16,2688]{1,0:T(8,128)(2,1)S(1)}, u32[]{:S(2)}, u32[]{:S(2)}) collective-permute-start(bf16[16,2688]{1,0:T(8,128)(2,1)S(1)} %get-tuple-element.27), channel_id=1, source_target_pairs={{0,16},{1,9},{2,18},{3,11},{4,20},{5,13},{6,22},{7,15},{8,24},{9,1... | collective-permute-start | bytes 258056 | tf_op jit(solution)/shard_map/ppermute | solution.py:50
  28.3 29.6 %collective-permute-start.8 = (bf16[512,2560]{1,0:T(8,128)(2,1)}, bf16[512,2560]{1,0:T(8,128)(2,1)}, u32[]{:S(2)}, u32[]{:S(2)}) collective-permute-start(bf16[512,2560]{1,0:T(8,128)(2,1)} %gate_a.1), channel_id=1, source_target_pairs={{0,1},{1,0},{2,3},{3,2},{4,5},{5,4},{6,7},{7,6},{8,9},{9,8},{10,11... | collective-permute-start | bytes 7864328 | tf_op jit(solution)/shard_map/ppermute | solution.py:30
  28.3 29.6 %collective-permute-start.9 = (bf16[512,2560]{1,0:T(8,128)(2,1)}, bf16[512,2560]{1,0:T(8,128)(2,1)}, u32[]{:S(2)}, u32[]{:S(2)}) collective-permute-start(bf16[512,2560]{1,0:T(8,128)(2,1)} %up_a.1), channel_id=1, source_target_pairs={{0,1},{1,0},{2,3},{3,2},{4,5},{5,4},{6,7},{7,6},{8,9},{9,8},{10,11... | collective-permute-start | bytes 7864328 | tf_op jit(solution)/shard_map/ppermute | solution.py:30
  28.8 29.1 %collective-permute-start.10 = (bf16[512,2560]{1,0:T(8,128)(2,1)}, bf16[512,2560]{1,0:T(8,128)(2,1)}, u32[]{:S(2)}, u32[]{:S(2)}) collective-permute-start(bf16[512,2560]{1,0:T(8,128)(2,1)} %down_a.1), channel_id=1, source_target_pairs={{0,1},{1,0},{2,3},{3,2},{4,5},{5,4},{6,7},{7,6},{8,9},{9,8},{10,11... | collective-permute-start | bytes 7864328 | tf_op jit(solution)/shard_map/ppermute | solution.py:30
  30.8 8.1 %collective-permute-start.6 = (bf16[32,2688]{1,0:T(8,128)(2,1)S(1)}, bf16[32,2688]{1,0:T(8,128)(2,1)S(1)}, u32[]{:S(2)}, u32[]{:S(2)}) collective-permute-start(bf16[32,2688]{1,0:T(8,128)(2,1)S(1)} %pad_maximum_fusion.1), channel_id=1, source_target_pairs={{0,8},{1,17},{2,10},{3,19},{4,12},{5,21},{6,14},{7,23},{8,0},{9,25... | collective-permute-start | bytes 516104 | tf_op jit(solution)/shard_map/ppermute | solution.py:50
  38.9 7.9 %collective-permute-start.7 = (bf16[64,2688]{1,0:T(8,128)(2,1)S(1)}, bf16[64,2688]{1,0:T(8,128)(2,1)S(1)}, u32[]{:S(2)}, u32[]{:S(2)}) collective-permute-start(bf16[64,2688]{1,0:T(8,128)(2,1)S(1)} %pad_maximum_fusion), channel_id=1, source_target_pairs={{0,4},{1,3},{2,6},{3,1},{4,0},{5,7},{6,2},{7,5},{8,12},{9,11},{10,... | collective-permute-start | bytes 1032200 | tf_op jit(solution)/shard_map/ppermute | solution.py:50
  46.9 11.0 %collective-permute-start.11 = (bf16[128,2688]{1,0:T(8,128)(2,1)S(1)}, bf16[128,2688]{1,0:T(8,128)(2,1)S(1)}, u32[]{:S(2)}, u32[]{:S(2)}) collective-permute-start(bf16[128,2688]{1,0:T(8,128)(2,1)S(1)} %constant_dynamic-update-slice_fusion.rows_ref), channel_id=1, source_target_pairs={{0,2},{1,5},{2,0},{3,7},{4,6},{5,1},{6,4},{7,3},{8,10},{9,13},{10,... | collective-permute-start | bytes 2064392 | tf_op jit(solution)/shard_map/ppermute | solution.py:50
  67.4 11.8 %collective-permute-start.12 = (bf16[128,2560]{1,0:T(8,128)(2,1)S(1)}, bf16[128,2560]{1,0:T(8,128)(2,1)S(1)}, u32[]{:S(2)}, u32[]{:S(2)}) collective-permute-start(bf16[128,2560]{1,0:T(8,128)(2,1)S(1)} %expert.3), channel_id=1, source_target_pairs={{0,2},{1,5},{2,0},{3,7},{4,6},{5,1},{6,4},{7,3},{8,10},{9,13},{10,... | collective-permute-start | bytes 1966088 | tf_op jit(solution)/shard_map/ppermute | solution.py:50
  79.4 7.6 %collective-permute-start.13 = (bf16[64,2560]{1,0:T(8,128)(2,1)S(1)}, bf16[64,2560]{1,0:T(8,128)(2,1)S(1)}, u32[]{:S(2)}, u32[]{:S(2)}) collective-permute-start(bf16[64,2560]{1,0:T(8,128)(2,1)S(1)} %slice.51), channel_id=1, source_target_pairs={{0,4},{1,3},{2,6},{3,1},{4,0},{5,7},{6,2},{7,5},{8,12},{9,11},{10,... | collective-permute-start | bytes 983048 | tf_op jit(solution)/shard_map/ppermute | solution.py:50
  87.1 9.4 %collective-permute-start.14 = (bf16[32,2560]{1,0:T(8,128)(2,1)S(1)}, bf16[32,2560]{1,0:T(8,128)(2,1)S(1)}, u32[]{:S(2)}, u32[]{:S(2)}) collective-permute-start(bf16[32,2560]{1,0:T(8,128)(2,1)S(1)} %slice.52), channel_id=1, source_target_pairs={{0,8},{1,17},{2,10},{3,19},{4,12},{5,21},{6,14},{7,23},{8,0},{9,25... | collective-permute-start | bytes 491528 | tf_op jit(solution)/shard_map/ppermute | solution.py:50
  96.6 6.8 %collective-permute-start.15 = (bf16[16,2560]{1,0:T(8,128)(2,1)S(1)}, bf16[16,2560]{1,0:T(8,128)(2,1)S(1)}, u32[]{:S(2)}, u32[]{:S(2)}) collective-permute-start(bf16[16,2560]{1,0:T(8,128)(2,1)S(1)} %slice.53), channel_id=1, source_target_pairs={{0,16},{1,9},{2,18},{3,11},{4,20},{5,13},{6,22},{7,15},{8,24},{9,1... | collective-permute-start | bytes 245768 | tf_op jit(solution)/shard_map/ppermute | solution.py:50
